TPU v7x, 32 devices: a whole 2x2x4 slice. The times are simulated.
32 devices in a mesh: groups: 1, rows: 16 (over z, y, core), cols: 2 (over x), sub: 1.
Axes of the slice: x: 2, y: 2, z: 4, core: 2. Of those that a mesh axis runs over, the one named last changes fastest.
Arguments:
- activations: bfloat16 [4096, 5376], P(('groups', 'rows'), ('cols', 'sub')), may hold values from -40 to 40
- positions: int32 [4096], P('groups'), may hold values from 0 to 6143, as said below
- query_weight: bfloat16 [5376, 4096], P('rows', ('cols', 'sub')), may hold values from -0.078125 to 0.078125
- key_weight: bfloat16 [5376, 2048], P('rows', ('cols', 'sub')), may hold values from -0.078125 to 0.078125
- value_weight: bfloat16 [5376, 2048], P('rows', ('cols', 'sub')), may hold values from -0.078125 to 0.078125
- output_weight: bfloat16 [4096, 5376], P(('cols', 'sub'), 'rows'), may hold values from -0.09375 to 0.09375
- input_gain: float32 [5376], replicated, may hold values from 0.1 to 1.9
- query_gain: float32 [128], replicated, may hold values from 0.1 to 1.9
- key_gain: float32 [128], replicated, may hold values from 0.1 to 1.9
Outputs:
- attended: bfloat16 [4096, 5376], P(('groups', 'rows'), ('cols', 'sub'))
Inputs may be any that keep to these rules, and one draw needn't show every extreme that they name: `positions`: position of each token in its document: it rises by one from token to token, or falls to 0 where a new document begins; the first document may begin at any position.
All inputs are finite; a program needn't handle non-finite values.
Results may differ from a plain program's by a relative error of at most 0.0065.
Values may be sent and summed in bfloat16 or wider, within the bound.
No kernel may reach another device: no remote copies, remote signals or barrier semaphores. Data moves between devices by JAX's collectives and lax.ppermute only.
A program may use at most 128 MiB of HBM per device.

v0:
```python
import functools
import math

import jax
import jax.numpy as jnp
from jax import lax
from jax.experimental import pallas as pl
from jax.experimental.pallas import tpu as pltpu
from jax.sharding import PartitionSpec as P


HD = 128
WINDOW = 1024
QUERY_SCALAR = 168
VMEM_BYTES = 67_000_000
AXES = ("rows", "cols", "sub")
ANY = pl.BlockSpec(memory_space=pl.ANY)
VMEM = pl.BlockSpec(memory_space=pltpu.VMEM)
SMEM = pl.BlockSpec(memory_space=pltpu.SMEM)


def passed_along(value, axis, by):
    peers = lax.axis_size(axis)
    pairs = [(i, i + by) for i in range(peers) if 0 <= i + by < peers]
    return lax.ppermute(value, axis, pairs)


def head_norm(tensor, gain_vector):
    return (
        tensor * lax.rsqrt(jnp.mean(tensor * tensor, axis=-1, keepdims=True) + 1e-06) * gain_vector
    )


def rotate(tensor, token_positions):
    half_width = tensor.shape[-1] // 2
    frequency = 10000.0 ** (-(jnp.arange(half_width, dtype=jnp.float32) * 2.0 / tensor.shape[-1]))
    angles = token_positions.astype(jnp.float32)[:, None] * frequency[None, :]
    cosine = jnp.cos(angles)[:, None, :]
    sine_part = jnp.sin(angles)[:, None, :]
    first_half = tensor[..., :half_width]
    second_half = tensor[..., half_width:]
    return jnp.concatenate(
        [
            first_half * cosine - second_half * sine_part,
            second_half * cosine + first_half * sine_part,
        ],
        axis=-1,
    )


def attend(queries, key_rows, value_rows, query_index, key_index, query_pos, key_pos):
    row_count = queries.shape[0]
    key_count = key_rows.shape[0]
    kv_heads = key_rows.shape[1] // HD
    group_size = queries.shape[1] // key_rows.shape[1]
    query_four = queries.reshape(row_count, kv_heads, group_size, HD)
    key_three = key_rows.reshape(key_count, kv_heads, HD)
    value_three = value_rows.reshape(key_count, kv_heads, HD)
    score_scale = 1.0 / math.sqrt(QUERY_SCALAR)
    scores = (
        jnp.einsum("qgrd,kgd->grqk", query_four, key_three, preferred_element_type=jnp.float32)
        * score_scale
    )
    distance = query_index[:, None] - key_index[None, :]
    visible = (
        (key_index[None, :] >= 0)
        & (distance >= 0)
        & (distance < WINDOW)
        & (query_pos[:, None] - key_pos[None, :] == distance)
    )
    weights = jnp.where(visible[None, None], jnp.exp(scores), 0.0)
    totals = jnp.sum(weights, axis=-1)
    rounded = weights.astype(jnp.bfloat16)
    mixed_heads = jnp.einsum(
        "grqk,kgd->qgrd", rounded, value_three, preferred_element_type=jnp.float32
    )
    mixed_heads = mixed_heads / jnp.transpose(totals, (2, 0, 1))[..., None]
    return mixed_heads.astype(jnp.bfloat16).reshape(row_count, kv_heads * group_size * HD)


def reach_back(key_rows, value_rows, reach_rows):
    pieces = []
    carried = (key_rows, value_rows)
    for _ in range(reach_rows):
        carried = passed_along((carried[0], carried[1]), "rows", 1)
        pieces.append(carried)
    ordered = pieces[::-1] + [(key_rows, value_rows)]
    all_keys = jnp.concatenate([member[0] for member in ordered], axis=0)
    all_values = jnp.concatenate([member[1] for member in ordered], axis=0)
    return (all_keys, all_values)


def gathered_body(
    activations,
    positions,
    query_weight,
    key_weight,
    value_weight,
    output_weight,
    input_gain,
    query_gain,
    key_gain,
):
    rows_here = activations.shape[0]
    row_panel = lax.all_gather(activations, ("cols", "sub"), axis=1, tiled=True)
    panel_wide = row_panel.astype(jnp.float32)
    inverse = lax.rsqrt(jnp.mean(panel_wide * panel_wide, axis=-1, keepdims=True) + 1e-06)
    normed = (panel_wide * inverse * input_gain).astype(jnp.bfloat16)
    row_index = lax.axis_index("rows")
    own_positions = lax.dynamic_slice_in_dim(positions, row_index * rows_here, rows_here, 0)
    reach_rows = min(-(-WINDOW // rows_here), lax.axis_size("rows") - 1)

    def add_rows(weight_piece):
        return jnp.dot(normed, weight_piece, preferred_element_type=jnp.float32)

    query_raw = add_rows(lax.all_gather(query_weight, "rows", axis=0, tiled=True))
    key_raw = add_rows(lax.all_gather(key_weight, "rows", axis=0, tiled=True))
    value_raw = add_rows(lax.all_gather(value_weight, "rows", axis=0, tiled=True))
    key_rows = rotate(head_norm(key_raw.reshape(rows_here, -1, HD), key_gain), own_positions)
    key_rows, value_rows = (
        key_rows.astype(jnp.bfloat16).reshape(rows_here, -1),
        value_raw.astype(jnp.bfloat16),
    )
    all_keys, all_values = reach_back(key_rows, value_rows, reach_rows)
    queries = rotate(head_norm(query_raw.reshape(rows_here, -1, HD), query_gain), own_positions)
    queries = queries.astype(jnp.bfloat16).reshape(rows_here, -1)
    key_count = all_keys.shape[0]
    query_index = row_index * rows_here + jnp.arange(rows_here, dtype=jnp.int32)
    key_index = (row_index - reach_rows) * rows_here + jnp.arange(key_count, dtype=jnp.int32)
    padded = jnp.concatenate([jnp.zeros((reach_rows * rows_here,), jnp.int32), positions], axis=0)
    key_positions = lax.dynamic_slice_in_dim(padded, row_index * rows_here, key_count, 0)
    context = attend(
        queries, all_keys, all_values, query_index, key_index, own_positions, key_positions
    )
    partial_terms = jnp.dot(
        context,
        lax.all_gather(output_weight, "rows", axis=1, tiled=True),
        preferred_element_type=jnp.float32,
    )
    summed = lax.psum_scatter(
        partial_terms.astype(jnp.bfloat16), ("cols", "sub"), scatter_dimension=1, tiled=True
    ).astype(jnp.float32)
    return (activations.astype(jnp.float32) + summed).astype(jnp.bfloat16)


def swapped(value, place=0, col=0):
    rows, cols = lax.axis_size("rows"), lax.axis_size("cols")
    pairs = [
        (r * cols + c, (r ^ place) * cols + (c ^ col)) for r in range(rows) for c in range(cols)
    ]
    return lax.ppermute(value, AXES, pairs)


def run(kernel, out_shape, in_specs, out_specs, scratch, flops, bytes_moved):
    return pl.pallas_call(
        kernel,
        out_shape=out_shape,
        in_specs=in_specs,
        out_specs=out_specs,
        scratch_shapes=scratch,
        compiler_params=pltpu.CompilerParams(vmem_limit_bytes=VMEM_BYTES),
        cost_estimate=pl.CostEstimate(
            flops=int(flops), bytes_accessed=int(bytes_moved), transcendentals=0
        ),
    )


def cut_kernel(n, meta, wq, wk, wv, *outs):
    place = meta[0]
    wide_q = wq.shape[1] // n
    wide_k = wk.shape[1] // n
    for m in range(n):
        at = lax.bitwise_xor(place, m)
        cols_k = pl.ds(pl.multiple_of(at * wide_k, 128), wide_k)
        cols_q = pl.ds(pl.multiple_of(at * wide_q, 128), wide_q)
        outs[m][:, :wide_k] = wk[:, cols_k]
        outs[m][:, wide_k:] = wv[:, cols_k]
        outs[n + m][...] = wq[:, cols_q]


def load_all(n, meta, blocks, weights, block_mem, weight_mem, block_sem, weight_sem):
    place, half = meta[0], meta[1]
    deep = weights[0].shape[0]
    copies = []
    for m in range(n):
        for far in range(2):
            owner = lax.bitwise_xor(place, m)
            rows = pl.ds(pl.multiple_of(owner * deep, 16), deep)
            copies.append(
                pltpu.make_async_copy(
                    weights[m * 2 + far],
                    weight_mem.at[lax.bitwise_xor(half, far), rows, :],
                    weight_sem.at[m * 2 + far],
                )
            )
    for copy in copies:
        copy.start()
    for m in range(n):
        for side in range(2):
            pltpu.make_async_copy(
                blocks[m * 2 + side], block_mem.at[m, side], block_sem.at[m, side]
            ).start()
    return copies


def project(m, meta, blocks, block_mem, weight_mem, block_sem):
    col = meta[2]
    for side in range(2):
        pltpu.make_async_copy(blocks[side], block_mem.at[m, side], block_sem.at[m, side]).wait()
    return jnp.dot(
        block_mem[m, 0], weight_mem[col], preferred_element_type=jnp.float32
    ) + jnp.dot(
        block_mem[m, 1], weight_mem[lax.bitwise_xor(col, 1)], preferred_element_type=jnp.float32
    )


def normed_rotated(raw, gain, cosine, sine):
    scaled = raw * lax.rsqrt(jnp.mean(raw * raw, axis=-1, keepdims=True) + 1e-06) * gain
    return scaled * cosine + pltpu.roll(scaled, HD // 2, 1) * sine


def key_kernel(n, reach, meta, cosine, sine, gain, *refs):
    blocks, weights = refs[: 2 * n], refs[2 * n : 4 * n]
    kv_out, tail_out, block_mem, weight_mem, block_sem, weight_sem = refs[4 * n :]
    copies = load_all(n, meta, blocks, weights, block_mem, weight_mem, block_sem, weight_sem)
    for copy in copies:
        copy.wait()
    place = meta[0]

    @pl.loop(0, n)
    def _(m):
        at = lax.bitwise_xor(place, m)
        raw = project(m, meta, blocks, block_mem, weight_mem, block_sem)
        keys = normed_rotated(raw[:, :HD], gain[...], cosine[at], sine[at]).astype(jnp.bfloat16)
        values = raw[:, HD:].astype(jnp.bfloat16)
        kv_out[m, :, :HD] = keys
        kv_out[m, :, HD:] = values

        @pl.when(at >= n - reach)
        def _():
            tail_out[at - (n - reach), :, :HD] = keys
            tail_out[at - (n - reach), :, HD:] = values


def attend_kernel(n, reach, heads, meta, cosine, sine, gain, q_doc, k_doc, kv_own, kv_back, *refs):
    blocks, weights = refs[: 2 * n], refs[2 * n : 4 * n]
    keep_out, send_out = refs[4 * n : 4 * n + 2]
    block_mem, weight_mem, kv_mem, block_sem, weight_sem, kv_sem = refs[4 * n + 2 :]
    place, col = meta[0], meta[2]
    tokens = block_mem.shape[2]
    part = tokens // 2
    copies = load_all(n, meta, blocks, weights, block_mem, weight_mem, block_sem, weight_sem)
    more = [pltpu.make_async_copy(kv_back, kv_mem.at[pl.ds(0, reach)], kv_sem.at[n])]
    for m in range(n):
        more.append(
            pltpu.make_async_copy(
                kv_own.at[m], kv_mem.at[reach + lax.bitwise_xor(place, m)], kv_sem.at[m]
            )
        )
    for copy in more:
        copy.start()
    for copy in copies + more:
        copy.wait()
    scale = 1.0 / math.sqrt(QUERY_SCALAR)
    row_at = lax.broadcasted_iota(jnp.int32, (tokens, tokens), 0)
    col_at = lax.broadcasted_iota(jnp.int32, (tokens, tokens), 1)

    @pl.loop(0, n)
    def _(m):
        at = lax.bitwise_xor(place, m)
        raw = project(m, meta, blocks, block_mem, weight_mem, block_sem)
        cosine_here, sine_here = cosine[at], sine[at]
        queries = [
            normed_rotated(
                raw[:, h * HD : (h + 1) * HD], gain[...], cosine_here, sine_here
            ).astype(jnp.bfloat16)
            for h in range(heads)
        ]
        doc = q_doc[at]
        totals = [jnp.zeros((tokens, 1), jnp.float32) for _ in range(heads)]
        mixed = [jnp.zeros((tokens, HD), jnp.float32) for _ in range(heads)]
        for step in range(reach + 1):
            pair = kv_mem[at + step]
            visible = doc == k_doc[at + step]
            if step == 0:
                visible = visible & (row_at < col_at)
            if step == reach:
                visible = visible & (row_at >= col_at)
            for h in range(heads):
                scores = lax.dot_general(
                    queries[h],
                    pair[:, :HD],
                    (((1,), (1,)), ((), ())),
                    preferred_element_type=jnp.float32,
                )
                weights_here = jnp.where(visible, jnp.exp(scores * scale), 0.0)
                totals[h] = totals[h] + jnp.sum(weights_here, axis=-1, keepdims=True)
                mixed[h] = mixed[h] + jnp.dot(
                    weights_here.astype(jnp.bfloat16),
                    pair[:, HD:],
                    preferred_element_type=jnp.float32,
                )
        for h in range(heads):
            done = (mixed[h] / totals[h]).astype(jnp.bfloat16)
            top, bottom = done[:part], done[part:]
            keep_out[at, :, h * HD : (h + 1) * HD] = jnp.where(col == 0, top, bottom)
            send_out[at, :, h * HD : (h + 1) * HD] = jnp.where(col == 0, bottom, top)


def output_kernel(n, meta, *refs):
    contexts, weights = refs[: 2 * n], refs[2 * n : 2 * n + 4]
    outs = refs[2 * n + 4 : 4 * n + 4]
    context_mem, weight_mem, result_mem, context_sem, weight_sem = refs[4 * n + 4 :]
    place, half, col = meta[0], meta[1], meta[2]
    deep = weights[0].shape[0]
    wide = contexts[0].shape[2]
    part = contexts[0].shape[1]
    copies = []
    for far in range(2):
        for side in range(2):
            rows = pl.ds(pl.multiple_of(lax.bitwise_xor(col, side) * deep, 16), deep)
            copies.append(
                pltpu.make_async_copy(
                    weights[far * 2 + side],
                    weight_mem.at[lax.bitwise_xor(half, far), rows, :],
                    weight_sem.at[far * 2 + side],
                )
            )
    for m in range(n):
        for side in range(2):
            first = lax.bitwise_xor(col, side) * deep + lax.bitwise_xor(place, m) * wide
            copies.append(
                pltpu.make_async_copy(
                    contexts[m * 2 + side],
                    context_mem.at[:, :, pl.ds(pl.multiple_of(first, 128), wide)],
                    context_sem.at[m * 2 + side],
                )
            )
    for copy in copies:
        copy.start()
    for copy in copies:
        copy.wait()

    @pl.loop(0, n // 2)
    def _(t):
        left = context_mem[pl.ds(2 * t, 2)].reshape(2 * part, 2 * deep)
        for block in range(2):
            result = jnp.dot(left, weight_mem[block], preferred_element_type=jnp.float32)
            result_mem[block, pl.ds(2 * t, 2)] = result.astype(jnp.bfloat16).reshape(2, part, -1)

    for m in range(n):
        for side in range(2):
            outs[m * 2 + side][...] = result_mem[
                lax.bitwise_xor(col, side), lax.bitwise_xor(place, m)
            ]


def split_body(
    activations,
    positions,
    query_weight,
    key_weight,
    value_weight,
    output_weight,
    input_gain,
    query_gain,
    key_gain,
):
    tokens, features = activations.shape
    n = key_weight.shape[1] // HD
    heads = query_weight.shape[1] // key_weight.shape[1]
    reach = WINDOW // tokens
    part = tokens // 2
    row = lax.axis_index("rows")
    col = lax.axis_index("cols")
    half, place = row // n, row % n
    meta = jnp.stack([place, half, col]).astype(jnp.int32)
    bf16, f32 = jnp.bfloat16, jnp.float32

    deep = query_weight.shape[0]
    pieces = run(
        functools.partial(cut_kernel, n),
        [jax.ShapeDtypeStruct((deep, 2 * HD), bf16)] * n
        + [jax.ShapeDtypeStruct((deep, heads * HD), bf16)] * n,
        [SMEM, VMEM, VMEM, VMEM],
        [VMEM] * (2 * n),
        [],
        0,
        4 * query_weight.size * 2,
    )(meta, query_weight, key_weight, value_weight)

    wide = activations.astype(f32)
    squares = jnp.sum(wide * wide, axis=-1).reshape(2, part)
    squares = (squares + swapped(squares, 0, 1)).reshape(tokens, 1)
    inverse = lax.rsqrt(squares / (2 * features) + 1e-06)
    gain = lax.dynamic_slice_in_dim(input_gain, col * features, features, 0)
    normed = (wide * inverse * gain).astype(bf16)

    z, y, c = n // 2, n // 4, 1
    blocks = {(0, 0): normed}
    blocks[z, 0] = swapped(normed, z, 0)
    blocks[y, 0] = swapped(normed, y, 0)
    blocks[0, 1] = swapped(normed, 0, 1)
    blocks[z + y, 0] = swapped(blocks[z, 0], y, 0)
    blocks[z, 1] = swapped(blocks[z, 0], 0, 1)
    blocks[y, 1] = swapped(blocks[y, 0], 0, 1)
    blocks[z + y, 1] = swapped(blocks[z, 1], y, 0)
    for m, side in list(blocks):
        blocks[m + c, side] = swapped(blocks[m, side], c, 0)
    block_list = [blocks[m, side] for m in range(n) for side in range(2)]

    def spread(mine):
        out = []
        for m in range(n):
            piece = mine[m] if m == 0 else swapped(mine[m], m, 0)
            out += [piece, swapped(piece, n, 0)]
        return out

    kv_weights = spread(pieces[:n])
    q_weights = spread(pieces[n:])

    in_half = lax.dynamic_slice_in_dim(positions, half * n * tokens, n * tokens, 0)
    frequency = 10000.0 ** (-(jnp.arange(HD // 2, dtype=f32) * 2.0 / HD))
    angles = in_half.astype(f32)[:, None] * frequency[None, :]
    cosine, sine = jnp.cos(angles), jnp.sin(angles)
    cosine = jnp.concatenate([cosine, cosine], -1).reshape(n, tokens, HD)
    sine = jnp.concatenate([-sine, sine], -1).reshape(n, tokens, HD)
    index = jnp.arange(positions.shape[0], dtype=jnp.int32)
    starts = jnp.concatenate(
        [jnp.full((reach * tokens,), -(2**30), jnp.int32), index - positions], 0
    )
    docs = lax.dynamic_slice_in_dim(starts, half * n * tokens, (n + reach) * tokens, 0)
    k_doc = docs.reshape(n + reach, 1, tokens)
    q_doc = docs[reach * tokens :].reshape(n, tokens, 1)

    block_bytes = 2 * n * tokens * features * 2
    stores = [
        pltpu.VMEM((n, 2, tokens, features), bf16),
        pltpu.VMEM((2, features, 2 * HD), bf16),
    ]
    sems = [pltpu.SemaphoreType.DMA((n, 2)), pltpu.SemaphoreType.DMA((2 * n,))]
    flops = 2 * n * tokens * 2 * features * 2 * HD
    kv_own, kv_tail = run(
        functools.partial(key_kernel, n, reach),
        [
            jax.ShapeDtypeStruct((n, tokens, 2 * HD), bf16),
            jax.ShapeDtypeStruct((reach, tokens, 2 * HD), bf16),
        ],
        [SMEM, VMEM, VMEM, VMEM] + [ANY] * (4 * n),
        [VMEM, VMEM],
        stores + sems,
        flops,
        block_bytes,
    )(meta, cosine, sine, key_gain.reshape(1, HD), *block_list, *kv_weights)
    kv_back = passed_along(kv_tail, "rows", n)

    context_shape = jax.ShapeDtypeStruct((n, part, heads * HD), bf16)
    keep, send = run(
        functools.partial(attend_kernel, n, reach, heads),
        [context_shape, context_shape],
        [SMEM, VMEM, VMEM, VMEM, VMEM, VMEM, ANY, ANY] + [ANY] * (4 * n),
        [VMEM, VMEM],
        stores
        + [pltpu.VMEM((n + reach, tokens, 2 * HD), bf16)]
        + sems
        + [pltpu.SemaphoreType.DMA((n + 1,))],
        2 * flops,
        block_bytes,
    )(
        meta,
        cosine,
        sine,
        query_gain.reshape(1, HD),
        q_doc,
        k_doc,
        kv_own,
        kv_back,
        *block_list,
        *q_weights,
    )

    out_far = swapped(output_weight, n, 0)
    out_weights = [output_weight, swapped(output_weight, 0, 1), out_far, swapped(out_far, 0, 1)]

    there = swapped(send, 0, 1)
    contexts = {(0, 0): keep, (0, 1): there}
    contexts[z, 0] = swapped(keep, z, 0)
    contexts[y, 0] = swapped(keep, y, 0)
    contexts[z + y, 0] = swapped(contexts[z, 0], y, 0)
    contexts[z, 1] = swapped(there, z, 0)
    contexts[y, 1] = swapped(there, y, 0)
    contexts[z + y, 1] = swapped(contexts[y, 1], z, 0)
    for m, side in list(contexts):
        contexts[m + c, side] = swapped(contexts[m, side], c, 0)
    context_list = [contexts[m, side] for m in range(n) for side in range(2)]

    out_cols = output_weight.shape[1]
    deep_out = output_weight.shape[0]
    results = run(
        functools.partial(output_kernel, n),
        [jax.ShapeDtypeStruct((part, out_cols), bf16)] * (2 * n),
        [SMEM] + [ANY] * (2 * n + 4),
        [VMEM] * (2 * n),
        [
            pltpu.VMEM((n, part, 2 * deep_out), bf16),
            pltpu.VMEM((2, 2 * deep_out, out_cols), bf16),
            pltpu.VMEM((2, n, part, out_cols), bf16),
            pltpu.SemaphoreType.DMA((2 * n,)),
            pltpu.SemaphoreType.DMA((4,)),
        ],
        2 * n * part * 2 * deep_out * 2 * out_cols,
        16 * deep_out * out_cols,
    )(meta, *context_list, *out_weights)

    arrived = [
        [
            results[m * 2 + side]
            if (m, side) == (0, 0)
            else swapped(results[m * 2 + side], m, side)
            for m in range(n)
        ]
        for side in range(2)
    ]
    lanes = []
    for side in range(2):
        ordered = arrived[side]
        bit = 1
        while bit < n:
            flip = (place & bit) != 0
            ordered = [jnp.where(flip, ordered[m ^ bit], ordered[m]) for m in range(n)]
            bit *= 2
        lanes.append(jnp.concatenate(ordered, axis=1))
    top = jnp.where(col == 0, lanes[0], lanes[1])
    bottom = jnp.where(col == 0, lanes[1], lanes[0])
    summed = jnp.concatenate([top, bottom], axis=0)
    return (wide + summed.astype(f32)).astype(bf16)


def fits(mesh, activations, key_weight):
    rows = mesh.shape["rows"]
    tokens = activations.shape[0] // (mesh.shape["groups"] * rows)
    splits = mesh.shape["cols"] * mesh.shape["sub"]
    n = key_weight.shape[1] // HD // splits
    return (
        mesh.shape["cols"] == 2
        and mesh.shape["sub"] == 1
        and n == 8
        and rows == 2 * n
        and WINDOW % tokens == 0
        and WINDOW // tokens <= n
        and tokens % 256 == 0
    )


def solution(mesh):
    placed = (
        P(("groups", "rows"), ("cols", "sub")),
        P("groups"),
        P("rows", ("cols", "sub")),
        P("rows", ("cols", "sub")),
        P("rows", ("cols", "sub")),
        P(("cols", "sub"), "rows"),
        P(),
        P(),
        P(),
    )

    def step(activations, positions, query_weight, key_weight, *rest):
        whole = not fits(mesh, activations, key_weight)

        def body(*args):
            if whole:
                return gathered_body(*args)
            return split_body(*args)

        return jax.shard_map(
            body,
            mesh=mesh,
            in_specs=placed,
            out_specs=P(("groups", "rows"), ("cols", "sub")),
            check_vma=False,
        )(activations, positions, query_weight, key_weight, *rest)

    return step
```

profile of v0, /device:TPU:0, one launch (start us, length us, event | category | flops | bytes accessed | tf_op | source)
XLA Modules:
  0.0 489.4 jit_solution(13074985476632945550)
XLA Ops:
  1.8 3.0 collective-permute-start
  7.9 2.1 collective-permute-start.8
  10.6 3.9 shard_map.91
  18.1 4.0 collective-permute-done.19.refs_20_
  26.5 18.4 %collective-permute-done.23.refs_24_ = bf16[336,256]{1,0:T(8,128)(2,1)S(1)} collective-permute-done((bf16[336,256]{1,0:T(8,128)(2,1)}, bf16[336,256]{1,0:T(8,128)(2,1)S(1)}, u32[]{:S(2)}, u32[]{:S(2)}) %collective-permute-start.23) | collective-permute-done | bytes 172064 | tf_op jit(solution)/shard_map/ppermute | solution.py:151
  44.9 3.9 collective-permute-start.16
  50.2 6.8 %collective-permute-done.27.refs_28_ = bf16[336,256]{1,0:T(8,128)(2,1)S(1)} collective-permute-done((bf16[336,256]{1,0:T(8,128)(2,1)}, bf16[336,256]{1,0:T(8,128)(2,1)S(1)}, u32[]{:S(2)}, u32[]{:S(2)}) %collective-permute-start.27) | collective-permute-done | bytes 172064 | tf_op jit(solution)/shard_map/ppermute | solution.py:151
  60.5 3.7 collective-permute-done.35.refs_20_
  64.3 2.9 collective-permute-start.20
  69.8 3.5 collective-permute-done.41.refs_26_
  73.9 8.6 %collective-permute-done.18.refs_19_ = bf16[336,256]{1,0:T(8,128)(2,1)S(1)} collective-permute-done((bf16[336,256]{1,0:T(8,128)(2,1)S(1)}, bf16[336,256]{1,0:T(8,128)(2,1)S(1)}, u32[]{:S(2)}, u32[]{:S(2)}) %collective-permute-start.18) | collective-permute-done | bytes 172064 | tf_op jit(solution)/shard_map/ppermute | solution.py:151
  84.2 2.1 collective-permute-done.20.refs_21_
  89.0 9.9 %collective-permute-done.24.refs_25_ = bf16[336,256]{1,0:T(8,128)(2,1)S(1)} collective-permute-done((bf16[336,256]{1,0:T(8,128)(2,1)S(1)}, bf16[336,256]{1,0:T(8,128)(2,1)S(1)}, u32[]{:S(2)}, u32[]{:S(2)}) %collective-permute-start.24) | collective-permute-done | bytes 172064 | tf_op jit(solution)/shard_map/ppermute | solution.py:151
  99.0 9.6 %collective-permute-done.26.refs_27_ = bf16[336,256]{1,0:T(8,128)(2,1)S(1)} collective-permute-done((bf16[336,256]{1,0:T(8,128)(2,1)S(1)}, bf16[336,256]{1,0:T(8,128)(2,1)S(1)}, u32[]{:S(2)}, u32[]{:S(2)}) %collective-permute-start.26) | collective-permute-done | bytes 172064 | tf_op jit(solution)/shard_map/ppermute | solution.py:151
  108.6 10.7 %collective-permute-done.28.refs_29_ = bf16[336,256]{1,0:T(8,128)(2,1)S(1)} collective-permute-done((bf16[336,256]{1,0:T(8,128)(2,1)S(1)}, bf16[336,256]{1,0:T(8,128)(2,1)S(1)}, u32[]{:S(2)}, u32[]{:S(2)}) %collective-permute-start.28) | collective-permute-done | bytes 172064 | tf_op jit(solution)/shard_map/ppermute | solution.py:151
  119.3 9.6 %collective-permute-done.30.refs_31_ = bf16[336,256]{1,0:T(8,128)(2,1)S(1)} collective-permute-done((bf16[336,256]{1,0:T(8,128)(2,1)S(1)}, bf16[336,256]{1,0:T(8,128)(2,1)S(1)}, u32[]{:S(2)}, u32[]{:S(2)}) %collective-permute-start.30) | collective-permute-done | bytes 172064 | tf_op jit(solution)/shard_map/ppermute | solution.py:151
  131.7 9.3 %collective-permute-done.9.refs_9_ = bf16[256,2688]{1,0:T(8,128)(2,1)S(1)} collective-permute-done((bf16[256,2688]{1,0:T(8,128)(2,1)}, bf16[256,2688]{1,0:T(8,128)(2,1)S(1)}, u32[]{:S(2)}, u32[]{:S(2)}) %collective-permute-start.9) | collective-permute-done | bytes 1376288 | tf_op jit(solution)/shard_map/ppermute | solution.py:151
  141.0 21.2 %collective-permute-done.12.refs_12_ = bf16[256,2688]{1,0:T(8,128)(2,1)} collective-permute-done((bf16[256,2688]{1,0:T(8,128)(2,1)}, bf16[256,2688]{1,0:T(8,128)(2,1)}, u32[]{:S(2)}, u32[]{:S(2)}) %collective-permute-start.12) | collective-permute-done | bytes 1376288 | tf_op jit(solution)/shard_map/ppermute | solution.py:151
  162.3 3.8 collective-permute-done.5.refs_5_
  166.7 24.1 %collective-permute-done.13.refs_13_ = bf16[256,2688]{1,0:T(8,128)(2,1)} collective-permute-done((bf16[256,2688]{1,0:T(8,128)(2,1)S(1)}, bf16[256,2688]{1,0:T(8,128)(2,1)}, u32[]{:S(2)}, u32[]{:S(2)}) %collective-permute-start.13) | collective-permute-done | bytes 1376288 | tf_op jit(solution)/shard_map/ppermute | solution.py:151
  191.0 3.7 fusion.4
  197.3 2.7 collective-permute-start.43
  200.1 2.6 collective-permute-start.32
  203.1 19.2 %shard_map.92 = (bf16[8,256,256]{2,1,0:T(8,128)(2,1)}, bf16[4,256,256]{2,1,0:T(8,128)(2,1)}) custom-call(s32[3]{0:T(128)} %pad_add_fusion.meta, f32[8,256,128]{2,1,0:T(8,128)} %pad_maximum_fusion.cosine, f32[8,256,128]{2,1,0:T(8,128)} %pad_maximum_fusion.1.sine, f32[1,128]{1,0:T(1,128)} %bitcast.12, bf16[256,2688]{1,0:T(8,128)(2,1)} %fusion.2.refs_0_, ...), custom_call_target="tpu_custom_call" | custom-call | flops 5637144576 | bytes 22020096 | tf_op jit(solution)/shard_map/pallas_call | solution.py:443
  222.3 3.3 collective-permute-done.43.refs_28_
  225.6 5.9 %collective-permute-start.31 = (bf16[4,256,256]{2,1,0:T(8,128)(2,1)}, bf16[4,256,256]{2,1,0:T(8,128)(2,1)}, u32[]{:S(2)}, u32[]{:S(2)}) collective-permute-start(bf16[4,256,256]{2,1,0:T(8,128)(2,1)} %get-tuple-element.50), channel_id=1, source_target_pairs={{0,16},{2,18},{4,20},{6,22},{8,24},{10,26},{12,28},{14,30},{1,17},... | collective-permute-start | bytes 1572872 | tf_op jit(solution)/shard_map/ppermute | solution.py:25
  232.0 36.8 %collective-permute-done.32.refs_17_ = bf16[336,256]{1,0:T(8,128)(2,1)} collective-permute-done((bf16[336,256]{1,0:T(8,128)(2,1)}, bf16[336,256]{1,0:T(8,128)(2,1)}, u32[]{:S(2)}, u32[]{:S(2)}) %collective-permute-start.32) | collective-permute-done | bytes 172064 | tf_op jit(solution)/shard_map/ppermute | solution.py:151
  268.8 3.7 collective-permute-done.34.refs_19_
  272.5 3.6 collective-permute-done.36.refs_21_
  276.1 3.7 collective-permute-done.38.refs_23_
  279.8 3.7 collective-permute-done.40.refs_25_
  290.9 3.6 collective-permute-done.46.refs_31_
  294.6 41.2 %shard_map.93 = (bf16[8,128,256]{2,1,0:T(8,128)(2,1)}, bf16[8,128,256]{2,1,0:T(8,128)(2,1)}) custom-call(s32[3]{0:T(128)} %pad_add_fusion.meta, f32[8,256,128]{2,1,0:T(8,128)} %pad_maximum_fusion.cosine, f32[8,256,128]{2,1,0:T(8,128)} %pad_maximum_fusion.1.sine, f32[1,128]{1,0:T(1,128)} %bitcast.13, s32[8,256,1]{2,1,0:T(8,128)} %slice.15.q_doc, ...), custom_call_target="tpu_custom_call" | custom-call | flops 11274289152 | bytes 22020096 | tf_op jit(solution)/shard_map/pallas_call | solution.py:458
  336.7 40.3 %collective-permute-start.54 = (bf16[8,128,256]{2,1,0:T(8,128)(2,1)}, bf16[8,128,256]{2,1,0:T(8,128)(2,1)S(1)}, u32[]{:S(2)}, u32[]{:S(2)}) collective-permute-start(bf16[8,128,256]{2,1,0:T(8,128)(2,1)} %get-tuple-element.59.refs_0_), channel_id=1, source_target_pairs={{0,8},{1,9},{2,10},{3,11},{4,12},{5,13},{6,14},{7,15},{8,0},{9,1},... | collective-permute-start | bytes 1572872 | tf_op jit(solution)/shard_map/ppermute | solution.py:151
  379.1 23.2 %collective-permute-start.55 = (bf16[8,128,256]{2,1,0:T(8,128)(2,1)S(1)}, bf16[8,128,256]{2,1,0:T(8,128)(2,1)S(1)}, u32[]{:S(2)}, u32[]{:S(2)}) collective-permute-start(bf16[8,128,256]{2,1,0:T(8,128)(2,1)S(1)} %collective-permute-done.47.refs_1_), channel_id=1, source_target_pairs={{0,8},{1,9},{2,10},{3,11},{4,12},{5,13},{6,14},{7,15},{8,0},{9,1},... | collective-permute-start | bytes 1572872 | tf_op jit(solution)/shard_map/ppermute | solution.py:151
  404.3 12.2 %collective-permute-start.59 = (bf16[8,128,256]{2,1,0:T(8,128)(2,1)S(1)}, bf16[8,128,256]{2,1,0:T(8,128)(2,1)S(1)}, u32[]{:S(2)}, u32[]{:S(2)}) collective-permute-start(bf16[8,128,256]{2,1,0:T(8,128)(2,1)S(1)} %collective-permute-done.51.refs_5_), channel_id=1, source_target_pairs={{0,8},{1,9},{2,10},{3,11},{4,12},{5,13},{6,14},{7,15},{8,0},{9,1},... | collective-permute-start | bytes 1572872 | tf_op jit(solution)/shard_map/ppermute | solution.py:151
  417.6 6.9 %collective-permute-done.59.refs_13_ = bf16[8,128,256]{2,1,0:T(8,128)(2,1)S(1)} collective-permute-done((bf16[8,128,256]{2,1,0:T(8,128)(2,1)S(1)}, bf16[8,128,256]{2,1,0:T(8,128)(2,1)S(1)}, u32[]{:S(2)}, u32[]{:S(2)}) %collective-permute-start.59) | collective-permute-done | bytes 524320 | tf_op jit(solution)/shard_map/ppermute | solution.py:151
  424.6 2.7 copy.18.refs_16_
  427.3 2.6 copy.20.refs_18_
  429.9 2.6 copy.19.refs_17_
  432.4 2.6 copy.21.refs_19_
  435.8 16.8 %shard_map.94 = (bf16[128,336]{1,0:T(8,128)(2,1)}, bf16[128,336]{1,0:T(8,128)(2,1)}, bf16[128,336]{1,0:T(8,128)(2,1)}, bf16[128,336]{1,0:T(8,128)(2,1)}, bf16[12...) custom-call(s32[3]{0:T(128)} %pad_add_fusion.meta, ...), custom_call_target="tpu_custom_call" | custom-call | flops 5637144576 | bytes 11010048 | tf_op jit(solution)/shard_map/pallas_call | solution.py:499
  452.6 2.5 collective-permute-start.65
  462.8 4.0 collective-permute-start.72
  471.5 2.5 collective-permute-start.77
  476.4 3.3 collective-permute-done.76
  479.7 2.3 collective-permute-done.77
  482.9 2.2 collective-permute-done.79
  (226 shorter events, 67.4 us)
Async XLA Ops:
  7.9 78.5 %collective-permute-start.8 = (bf16[256,2688]{1,0:T(8,128)(2,1)}, bf16[256,2688]{1,0:T(8,128)(2,1)}, u32[]{:S(2)}, u32[]{:S(2)}) collective-permute-start(bf16[256,2688]{1,0:T(8,128)(2,1)} %fusion.2.refs_0_), channel_id=1, source_target_pairs={{0,8},{1,9},{2,10},{3,11},{4,12},{5,13},{6,14},{7,15},{8,0},{9,1},... | collective-permute-start | bytes 4128776 | tf_op jit(solution)/shard_map/ppermute | solution.py:151
  16.4 28.5 %collective-permute-start.23 = (bf16[336,256]{1,0:T(8,128)(2,1)}, bf16[336,256]{1,0:T(8,128)(2,1)S(1)}, u32[]{:S(2)}, u32[]{:S(2)}) collective-permute-start(bf16[336,256]{1,0:T(8,128)(2,1)} %get-tuple-element.45), channel_id=1, source_target_pairs={{0,8},{1,9},{2,10},{3,11},{4,12},{5,13},{6,14},{7,15},{8,0},{9,1},... | collective-permute-start | bytes 516104 | tf_op jit(solution)/shard_map/ppermute | solution.py:151
  16.6 32.2 %collective-permute-start.25 = (bf16[336,256]{1,0:T(8,128)(2,1)}, bf16[336,256]{1,0:T(8,128)(2,1)S(1)}, u32[]{:S(2)}, u32[]{:S(2)}) collective-permute-start(bf16[336,256]{1,0:T(8,128)(2,1)} %get-tuple-element.46), channel_id=1, source_target_pairs={{0,10},{1,11},{2,8},{3,9},{4,14},{5,15},{6,12},{7,13},{8,2},{9,3},... | collective-permute-start | bytes 516104 | tf_op jit(solution)/shard_map/ppermute | solution.py:151
  22.1 34.9 %collective-permute-start.27 = (bf16[336,256]{1,0:T(8,128)(2,1)}, bf16[336,256]{1,0:T(8,128)(2,1)S(1)}, u32[]{:S(2)}, u32[]{:S(2)}) collective-permute-start(bf16[336,256]{1,0:T(8,128)(2,1)} %get-tuple-element.47), channel_id=1, source_target_pairs={{0,12},{1,13},{2,14},{3,15},{4,8},{5,9},{6,10},{7,11},{8,4},{9,5},... | collective-permute-start | bytes 516104 | tf_op jit(solution)/shard_map/ppermute | solution.py:151
  24.7 32.7 %collective-permute-start.29 = (bf16[336,256]{1,0:T(8,128)(2,1)}, bf16[336,256]{1,0:T(8,128)(2,1)S(1)}, u32[]{:S(2)}, u32[]{:S(2)}) collective-permute-start(bf16[336,256]{1,0:T(8,128)(2,1)} %get-tuple-element.48), channel_id=1, source_target_pairs={{0,14},{1,15},{2,12},{3,13},{4,10},{5,11},{6,8},{7,9},{8,6},{9,7},... | collective-permute-start | bytes 516104 | tf_op jit(solution)/shard_map/ppermute | solution.py:151
  44.9 13.7 %collective-permute-start.16 = (bf16[336,256]{1,0:T(8,128)(2,1)}, bf16[336,256]{1,0:T(8,128)(2,1)S(1)}, u32[]{:S(2)}, u32[]{:S(2)}) collective-permute-start(bf16[336,256]{1,0:T(8,128)(2,1)} %get-tuple-element.41.refs_16_), channel_id=1, source_target_pairs={{0,16},{1,17},{2,18},{3,19},{4,20},{5,21},{6,22},{7,23},{8,24},{9,... | collective-permute-start | bytes 516104 | tf_op jit(solution)/shard_map/ppermute | solution.py:151
  48.8 11.6 %collective-permute-start.33 = (bf16[336,256]{1,0:T(8,128)(2,1)}, bf16[336,256]{1,0:T(8,128)(2,1)}, u32[]{:S(2)}, u32[]{:S(2)}) collective-permute-start(bf16[336,256]{1,0:T(8,128)(2,1)} %get-tuple-element.52), channel_id=1, source_target_pairs={{0,2},{1,3},{2,0},{3,1},{4,6},{5,7},{6,4},{7,5},{8,10},{9,11},{10,... | collective-permute-start | bytes 516104 | tf_op jit(solution)/shard_map/ppermute | solution.py:151
  60.4 12.9 %collective-permute-start.41 = (bf16[336,256]{1,0:T(8,128)(2,1)}, bf16[336,256]{1,0:T(8,128)(2,1)}, u32[]{:S(2)}, u32[]{:S(2)}) collective-permute-start(bf16[336,256]{1,0:T(8,128)(2,1)} %get-tuple-element.56), channel_id=1, source_target_pairs={{0,10},{1,11},{2,8},{3,9},{4,14},{5,15},{6,12},{7,13},{8,2},{9,3},... | collective-permute-start | bytes 516104 | tf_op jit(solution)/shard_map/ppermute | solution.py:151
  64.3 18.3 %collective-permute-start.18 = (bf16[336,256]{1,0:T(8,128)(2,1)S(1)}, bf16[336,256]{1,0:T(8,128)(2,1)S(1)}, u32[]{:S(2)}, u32[]{:S(2)}) collective-permute-start(bf16[336,256]{1,0:T(8,128)(2,1)S(1)} %collective-permute-done.17.refs_18_), channel_id=1, source_target_pairs={{0,16},{1,17},{2,18},{3,19},{4,20},{5,21},{6,22},{7,23},{8,24},{9,... | collective-permute-start | bytes 516104 | tf_op jit(solution)/shard_map/ppermute | solution.py:151
  64.3 22.0 %collective-permute-start.20 = (bf16[336,256]{1,0:T(8,128)(2,1)S(1)}, bf16[336,256]{1,0:T(8,128)(2,1)}, u32[]{:S(2)}, u32[]{:S(2)}) collective-permute-start(bf16[336,256]{1,0:T(8,128)(2,1)S(1)} %collective-permute-done.19.refs_20_), channel_id=1, source_target_pairs={{0,16},{1,17},{2,18},{3,19},{4,20},{5,21},{6,22},{7,23},{8,24},{9,... | collective-permute-start | bytes 516104 | tf_op jit(solution)/shard_map/ppermute | solution.py:151
  67.9 21.1 %collective-permute-start.22 = (bf16[336,256]{1,0:T(8,128)(2,1)S(1)}, bf16[336,256]{1,0:T(8,128)(2,1)S(1)}, u32[]{:S(2)}, u32[]{:S(2)}) collective-permute-start(bf16[336,256]{1,0:T(8,128)(2,1)S(1)} %collective-permute-done.21.refs_22_), channel_id=1, source_target_pairs={{0,16},{1,17},{2,18},{3,19},{4,20},{5,21},{6,22},{7,23},{8,24},{9,... | collective-permute-start | bytes 516104 | tf_op jit(solution)/shard_map/ppermute | solution.py:151
  73.3 56.2 %collective-permute-start.4 = (bf16[256,2688]{1,0:T(8,128)(2,1)}, bf16[256,2688]{1,0:T(8,128)(2,1)S(1)}, u32[]{:S(2)}, u32[]{:S(2)}) collective-permute-start(bf16[256,2688]{1,0:T(8,128)(2,1)} %fusion.2.refs_0_), channel_id=1, source_target_pairs={{0,4},{1,5},{2,6},{3,7},{4,0},{5,1},{6,2},{7,3},{8,12},{9,13},{10,... | collective-permute-start | bytes 4128776 | tf_op jit(solution)/shard_map/ppermute | solution.py:151
  82.5 48.5 %collective-permute-start.1 = (bf16[256,2688]{1,0:T(8,128)(2,1)}, bf16[256,2688]{1,0:T(8,128)(2,1)S(1)}, u32[]{:S(2)}, u32[]{:S(2)}) collective-permute-start(bf16[256,2688]{1,0:T(8,128)(2,1)} %fusion.2.refs_0_), channel_id=1, source_target_pairs={{0,1},{1,0},{2,3},{3,2},{4,5},{5,4},{6,7},{7,6},{8,9},{9,8},{10,11... | collective-permute-start | bytes 4128776 | tf_op jit(solution)/shard_map/ppermute | solution.py:151
  86.3 44.8 %collective-permute-start.2 = (bf16[256,2688]{1,0:T(8,128)(2,1)}, bf16[256,2688]{1,0:T(8,128)(2,1)S(1)}, u32[]{:S(2)}, u32[]{:S(2)}) collective-permute-start(bf16[256,2688]{1,0:T(8,128)(2,1)} %fusion.2.refs_0_), channel_id=1, source_target_pairs={{0,2},{1,3},{2,0},{3,1},{4,6},{5,7},{6,4},{7,5},{8,10},{9,11},{10,... | collective-permute-start | bytes 4128776 | tf_op jit(solution)/shard_map/ppermute | solution.py:151
  86.3 54.7 %collective-permute-start.9 = (bf16[256,2688]{1,0:T(8,128)(2,1)}, bf16[256,2688]{1,0:T(8,128)(2,1)S(1)}, u32[]{:S(2)}, u32[]{:S(2)}) collective-permute-start(bf16[256,2688]{1,0:T(8,128)(2,1)} %collective-permute-done.8.refs_8_), channel_id=1, source_target_pairs={{0,1},{1,0},{2,3},{3,2},{4,5},{5,4},{6,7},{7,6},{8,9},{9,8},{10,11... | collective-permute-start | bytes 4128776 | tf_op jit(solution)/shard_map/ppermute | solution.py:151
  128.9 33.4 %collective-permute-start.12 = (bf16[256,2688]{1,0:T(8,128)(2,1)}, bf16[256,2688]{1,0:T(8,128)(2,1)}, u32[]{:S(2)}, u32[]{:S(2)}) collective-permute-start(bf16[256,2688]{1,0:T(8,128)(2,1)} %collective-permute-done.8.refs_8_), channel_id=1, source_target_pairs={{0,4},{1,5},{2,6},{3,7},{4,0},{5,1},{6,2},{7,3},{8,12},{9,13},{10,... | collective-permute-start | bytes 4128776 | tf_op jit(solution)/shard_map/ppermute | solution.py:151
  129.5 36.5 %collective-permute-start.5 = (bf16[256,2688]{1,0:T(8,128)(2,1)S(1)}, bf16[256,2688]{1,0:T(8,128)(2,1)}, u32[]{:S(2)}, u32[]{:S(2)}) collective-permute-start(bf16[256,2688]{1,0:T(8,128)(2,1)S(1)} %collective-permute-done.4.refs_4_), channel_id=1, source_target_pairs={{0,1},{1,0},{2,3},{3,2},{4,5},{5,4},{6,7},{7,6},{8,9},{9,8},{10,11... | collective-permute-start | bytes 4128776 | tf_op jit(solution)/shard_map/ppermute | solution.py:151
  131.0 35.0 %collective-permute-start.10 = (bf16[256,2688]{1,0:T(8,128)(2,1)}, bf16[256,2688]{1,0:T(8,128)(2,1)S(1)}, u32[]{:S(2)}, u32[]{:S(2)}) collective-permute-start(bf16[256,2688]{1,0:T(8,128)(2,1)} %collective-permute-done.8.refs_8_), channel_id=1, source_target_pairs={{0,2},{1,3},{2,0},{3,1},{4,6},{5,7},{6,4},{7,5},{8,10},{9,11},{10,... | collective-permute-start | bytes 4128776 | tf_op jit(solution)/shard_map/ppermute | solution.py:151
  131.2 35.4 %collective-permute-start.6 = (bf16[256,2688]{1,0:T(8,128)(2,1)S(1)}, bf16[256,2688]{1,0:T(8,128)(2,1)S(1)}, u32[]{:S(2)}, u32[]{:S(2)}) collective-permute-start(bf16[256,2688]{1,0:T(8,128)(2,1)S(1)} %collective-permute-done.4.refs_4_), channel_id=1, source_target_pairs={{0,2},{1,3},{2,0},{3,1},{4,6},{5,7},{6,4},{7,5},{8,10},{9,11},{10,... | collective-permute-start | bytes 4128776 | tf_op jit(solution)/shard_map/ppermute | solution.py:151
  141.0 49.8 %collective-permute-start.13 = (bf16[256,2688]{1,0:T(8,128)(2,1)S(1)}, bf16[256,2688]{1,0:T(8,128)(2,1)}, u32[]{:S(2)}, u32[]{:S(2)}) collective-permute-start(bf16[256,2688]{1,0:T(8,128)(2,1)S(1)} %collective-permute-done.9.refs_9_), channel_id=1, source_target_pairs={{0,4},{1,5},{2,6},{3,7},{4,0},{5,1},{6,2},{7,3},{8,12},{9,13},{10,... | collective-permute-start | bytes 4128776 | tf_op jit(solution)/shard_map/ppermute | solution.py:151
  162.3 28.6 %collective-permute-start.3 = (bf16[256,2688]{1,0:T(8,128)(2,1)S(1)}, bf16[256,2688]{1,0:T(8,128)(2,1)}, u32[]{:S(2)}, u32[]{:S(2)}) collective-permute-start(bf16[256,2688]{1,0:T(8,128)(2,1)S(1)} %collective-permute-done.1.refs_1_), channel_id=1, source_target_pairs={{0,2},{1,3},{2,0},{3,1},{4,6},{5,7},{6,4},{7,5},{8,10},{9,11},{10,... | collective-permute-start | bytes 4128776 | tf_op jit(solution)/shard_map/ppermute | solution.py:151
  166.1 31.3 %collective-permute-start.11 = (bf16[256,2688]{1,0:T(8,128)(2,1)S(1)}, bf16[256,2688]{1,0:T(8,128)(2,1)}, u32[]{:S(2)}, u32[]{:S(2)}) collective-permute-start(bf16[256,2688]{1,0:T(8,128)(2,1)S(1)} %collective-permute-done.9.refs_9_), channel_id=1, source_target_pairs={{0,2},{1,3},{2,0},{3,1},{4,6},{5,7},{6,4},{7,5},{8,10},{9,11},{10,... | collective-permute-start | bytes 4128776 | tf_op jit(solution)/shard_map/ppermute | solution.py:151
  166.1 34.0 %collective-permute-start.14 = (bf16[256,2688]{1,0:T(8,128)(2,1)}, bf16[256,2688]{1,0:T(8,128)(2,1)}, u32[]{:S(2)}, u32[]{:S(2)}) collective-permute-start(bf16[256,2688]{1,0:T(8,128)(2,1)} %collective-permute-done.12.refs_12_), channel_id=1, source_target_pairs={{0,2},{1,3},{2,0},{3,1},{4,6},{5,7},{6,4},{7,5},{8,10},{9,11},{10,... | collective-permute-start | bytes 4128776 | tf_op jit(solution)/shard_map/ppermute | solution.py:151
  166.6 33.5 %collective-permute-start.7 = (bf16[256,2688]{1,0:T(8,128)(2,1)}, bf16[256,2688]{1,0:T(8,128)(2,1)}, u32[]{:S(2)}, u32[]{:S(2)}) collective-permute-start(bf16[256,2688]{1,0:T(8,128)(2,1)} %collective-permute-done.5.refs_5_), channel_id=1, source_target_pairs={{0,2},{1,3},{2,0},{3,1},{4,6},{5,7},{6,4},{7,5},{8,10},{9,11},{10,... | collective-permute-start | bytes 4128776 | tf_op jit(solution)/shard_map/ppermute | solution.py:151
  190.8 11.9 %collective-permute-start.15 = (bf16[256,2688]{1,0:T(8,128)(2,1)}, bf16[256,2688]{1,0:T(8,128)(2,1)}, u32[]{:S(2)}, u32[]{:S(2)}) collective-permute-start(bf16[256,2688]{1,0:T(8,128)(2,1)} %collective-permute-done.13.refs_13_), channel_id=1, source_target_pairs={{0,2},{1,3},{2,0},{3,1},{4,6},{5,7},{6,4},{7,5},{8,10},{9,11},{10,... | collective-permute-start | bytes 4128776 | tf_op jit(solution)/shard_map/ppermute | solution.py:151
  190.9 97.0 %collective-permute-start.63 = (bf16[2048,336]{0,1:T(8,128)(2,1)}, bf16[2048,336]{0,1:T(8,128)(2,1)}, u32[]{:S(2)}, u32[]{:S(2)}) collective-permute-start(bf16[2048,336]{0,1:T(8,128)(2,1)} %param.14), channel_id=1, source_target_pairs={{0,16},{1,17},{2,18},{3,19},{4,20},{5,21},{6,22},{7,23},{8,24},{9,... | collective-permute-start | bytes 4128776 | tf_op jit(solution)/shard_map/ppermute | solution.py:151
  197.3 28.2 %collective-permute-start.43 = (bf16[336,256]{1,0:T(8,128)(2,1)}, bf16[336,256]{1,0:T(8,128)(2,1)}, u32[]{:S(2)}, u32[]{:S(2)}) collective-permute-start(bf16[336,256]{1,0:T(8,128)(2,1)} %get-tuple-element.57), channel_id=1, source_target_pairs={{0,12},{1,13},{2,14},{3,15},{4,8},{5,9},{6,10},{7,11},{8,4},{9,5},... | collective-permute-start | bytes 516104 | tf_op jit(solution)/shard_map/ppermute | solution.py:151
  200.1 31.4 %collective-permute-start.45 = (bf16[336,256]{1,0:T(8,128)(2,1)}, bf16[336,256]{1,0:T(8,128)(2,1)}, u32[]{:S(2)}, u32[]{:S(2)}) collective-permute-start(bf16[336,256]{1,0:T(8,128)(2,1)} %get-tuple-element.58), channel_id=1, source_target_pairs={{0,14},{1,15},{2,12},{3,13},{4,10},{5,11},{6,8},{7,9},{8,6},{9,7},... | collective-permute-start | bytes 516104 | tf_op jit(solution)/shard_map/ppermute | solution.py:151
  200.1 68.7 %collective-permute-start.32 = (bf16[336,256]{1,0:T(8,128)(2,1)}, bf16[336,256]{1,0:T(8,128)(2,1)}, u32[]{:S(2)}, u32[]{:S(2)}) collective-permute-start(bf16[336,256]{1,0:T(8,128)(2,1)} %get-tuple-element.51.refs_16_), channel_id=1, source_target_pairs={{0,16},{1,17},{2,18},{3,19},{4,20},{5,21},{6,22},{7,23},{8,24},{9,... | collective-permute-start | bytes 516104 | tf_op jit(solution)/shard_map/ppermute | solution.py:151
  202.7 69.8 %collective-permute-start.34 = (bf16[336,256]{1,0:T(8,128)(2,1)}, bf16[336,256]{1,0:T(8,128)(2,1)}, u32[]{:S(2)}, u32[]{:S(2)}) collective-permute-start(bf16[336,256]{1,0:T(8,128)(2,1)} %collective-permute-done.33.refs_18_), channel_id=1, source_target_pairs={{0,16},{1,17},{2,18},{3,19},{4,20},{5,21},{6,22},{7,23},{8,24},{9,... | collective-permute-start | bytes 516104 | tf_op jit(solution)/shard_map/ppermute | solution.py:151
  225.6 69.0 %collective-permute-start.31 = (bf16[4,256,256]{2,1,0:T(8,128)(2,1)}, bf16[4,256,256]{2,1,0:T(8,128)(2,1)}, u32[]{:S(2)}, u32[]{:S(2)}) collective-permute-start(bf16[4,256,256]{2,1,0:T(8,128)(2,1)} %get-tuple-element.50), channel_id=1, source_target_pairs={{0,16},{2,18},{4,20},{6,22},{8,24},{10,26},{12,28},{14,30},{1,17},... | collective-permute-start | bytes 1572872 | tf_op jit(solution)/shard_map/ppermute | solution.py:25
  231.5 44.6 %collective-permute-start.36 = (bf16[336,256]{1,0:T(8,128)(2,1)}, bf16[336,256]{1,0:T(8,128)(2,1)S(1)}, u32[]{:S(2)}, u32[]{:S(2)}) collective-permute-start(bf16[336,256]{1,0:T(8,128)(2,1)} %copy-done.34), channel_id=1, source_target_pairs={{0,16},{1,17},{2,18},{3,19},{4,20},{5,21},{6,22},{7,23},{8,24},{9,... | collective-permute-start | bytes 516104 | tf_op jit(solution)/shard_map/ppermute | solution.py:151
  287.2 90.3 %collective-permute-start.62 = (bf16[2048,336]{0,1:T(8,128)(2,1)}, bf16[2048,336]{0,1:T(8,128)(2,1)}, u32[]{:S(2)}, u32[]{:S(2)}) collective-permute-start(bf16[2048,336]{0,1:T(8,128)(2,1)} %param.14), channel_id=1, source_target_pairs={{0,1},{1,0},{2,3},{3,2},{4,5},{5,4},{6,7},{7,6},{8,9},{9,8},{10,11... | collective-permute-start | bytes 4128776 | tf_op jit(solution)/shard_map/ppermute | solution.py:151
  287.9 91.2 %collective-permute-start.64 = (bf16[2048,336]{0,1:T(8,128)(2,1)}, bf16[2048,336]{0,1:T(8,128)(2,1)}, u32[]{:S(2)}, u32[]{:S(2)}) collective-permute-start(bf16[2048,336]{0,1:T(8,128)(2,1)} %collective-permute-done.63), channel_id=1, source_target_pairs={{0,1},{1,0},{2,3},{3,2},{4,5},{5,4},{6,7},{7,6},{8,9},{9,8},{10,11... | collective-permute-start | bytes 4128776 | tf_op jit(solution)/shard_map/ppermute | solution.py:151
  335.8 41.6 %collective-permute-start.47 = (bf16[8,128,256]{2,1,0:T(8,128)(2,1)}, bf16[8,128,256]{2,1,0:T(8,128)(2,1)S(1)}, u32[]{:S(2)}, u32[]{:S(2)}) collective-permute-start(bf16[8,128,256]{2,1,0:T(8,128)(2,1)} %get-tuple-element.60), channel_id=1, source_target_pairs={{0,1},{1,0},{2,3},{3,2},{4,5},{5,4},{6,7},{7,6},{8,9},{9,8},{10,11... | collective-permute-start | bytes 1572872 | tf_op jit(solution)/shard_map/ppermute | solution.py:151
  336.7 65.6 %collective-permute-start.54 = (bf16[8,128,256]{2,1,0:T(8,128)(2,1)}, bf16[8,128,256]{2,1,0:T(8,128)(2,1)S(1)}, u32[]{:S(2)}, u32[]{:S(2)}) collective-permute-start(bf16[8,128,256]{2,1,0:T(8,128)(2,1)} %get-tuple-element.59.refs_0_), channel_id=1, source_target_pairs={{0,8},{1,9},{2,10},{3,11},{4,12},{5,13},{6,14},{7,15},{8,0},{9,1},... | collective-permute-start | bytes 1572872 | tf_op jit(solution)/shard_map/ppermute | solution.py:151
  377.0 26.7 %collective-permute-start.50 = (bf16[8,128,256]{2,1,0:T(8,128)(2,1)}, bf16[8,128,256]{2,1,0:T(8,128)(2,1)S(1)}, u32[]{:S(2)}, u32[]{:S(2)}) collective-permute-start(bf16[8,128,256]{2,1,0:T(8,128)(2,1)} %get-tuple-element.59.refs_0_), channel_id=1, source_target_pairs={{0,4},{1,5},{2,6},{3,7},{4,0},{5,1},{6,2},{7,3},{8,12},{9,13},{10,... | collective-permute-start | bytes 1572872 | tf_op jit(solution)/shard_map/ppermute | solution.py:151
  377.4 26.4 %collective-permute-start.48 = (bf16[8,128,256]{2,1,0:T(8,128)(2,1)}, bf16[8,128,256]{2,1,0:T(8,128)(2,1)S(1)}, u32[]{:S(2)}, u32[]{:S(2)}) collective-permute-start(bf16[8,128,256]{2,1,0:T(8,128)(2,1)} %get-tuple-element.59.refs_0_), channel_id=1, source_target_pairs={{0,2},{1,3},{2,0},{3,1},{4,6},{5,7},{6,4},{7,5},{8,10},{9,11},{10,... | collective-permute-start | bytes 1572872 | tf_op jit(solution)/shard_map/ppermute | solution.py:151
  377.5 26.8 %collective-permute-start.51 = (bf16[8,128,256]{2,1,0:T(8,128)(2,1)S(1)}, bf16[8,128,256]{2,1,0:T(8,128)(2,1)S(1)}, u32[]{:S(2)}, u32[]{:S(2)}) collective-permute-start(bf16[8,128,256]{2,1,0:T(8,128)(2,1)S(1)} %collective-permute-done.47.refs_1_), channel_id=1, source_target_pairs={{0,4},{1,5},{2,6},{3,7},{4,0},{5,1},{6,2},{7,3},{8,12},{9,13},{10,... | collective-permute-start | bytes 1572872 | tf_op jit(solution)/shard_map/ppermute | solution.py:151
  379.1 37.3 %collective-permute-start.55 = (bf16[8,128,256]{2,1,0:T(8,128)(2,1)S(1)}, bf16[8,128,256]{2,1,0:T(8,128)(2,1)S(1)}, u32[]{:S(2)}, u32[]{:S(2)}) collective-permute-start(bf16[8,128,256]{2,1,0:T(8,128)(2,1)S(1)} %collective-permute-done.47.refs_1_), channel_id=1, source_target_pairs={{0,8},{1,9},{2,10},{3,11},{4,12},{5,13},{6,14},{7,15},{8,0},{9,1},... | collective-permute-start | bytes 1572872 | tf_op jit(solution)/shard_map/ppermute | solution.py:151
  402.3 14.2 %collective-permute-start.58 = (bf16[8,128,256]{2,1,0:T(8,128)(2,1)S(1)}, bf16[8,128,256]{2,1,0:T(8,128)(2,1)S(1)}, u32[]{:S(2)}, u32[]{:S(2)}) collective-permute-start(bf16[8,128,256]{2,1,0:T(8,128)(2,1)S(1)} %collective-permute-done.54.refs_8_), channel_id=1, source_target_pairs={{0,4},{1,5},{2,6},{3,7},{4,0},{5,1},{6,2},{7,3},{8,12},{9,13},{10,... | collective-permute-start | bytes 1572872 | tf_op jit(solution)/shard_map/ppermute | solution.py:151
  403.7 13.3 %collective-permute-start.49 = (bf16[8,128,256]{2,1,0:T(8,128)(2,1)S(1)}, bf16[8,128,256]{2,1,0:T(8,128)(2,1)S(1)}, u32[]{:S(2)}, u32[]{:S(2)}) collective-permute-start(bf16[8,128,256]{2,1,0:T(8,128)(2,1)S(1)} %collective-permute-done.47.refs_1_), channel_id=1, source_target_pairs={{0,2},{1,3},{2,0},{3,1},{4,6},{5,7},{6,4},{7,5},{8,10},{9,11},{10,... | collective-permute-start | bytes 1572872 | tf_op jit(solution)/shard_map/ppermute | solution.py:151
  403.8 13.3 %collective-permute-start.52 = (bf16[8,128,256]{2,1,0:T(8,128)(2,1)S(1)}, bf16[8,128,256]{2,1,0:T(8,128)(2,1)S(1)}, u32[]{:S(2)}, u32[]{:S(2)}) collective-permute-start(bf16[8,128,256]{2,1,0:T(8,128)(2,1)S(1)} %collective-permute-done.50.refs_4_), channel_id=1, source_target_pairs={{0,2},{1,3},{2,0},{3,1},{4,6},{5,7},{6,4},{7,5},{8,10},{9,11},{10,... | collective-permute-start | bytes 1572872 | tf_op jit(solution)/shard_map/ppermute | solution.py:151
  404.3 20.2 %collective-permute-start.59 = (bf16[8,128,256]{2,1,0:T(8,128)(2,1)S(1)}, bf16[8,128,256]{2,1,0:T(8,128)(2,1)S(1)}, u32[]{:S(2)}, u32[]{:S(2)}) collective-permute-start(bf16[8,128,256]{2,1,0:T(8,128)(2,1)S(1)} %collective-permute-done.51.refs_5_), channel_id=1, source_target_pairs={{0,8},{1,9},{2,10},{3,11},{4,12},{5,13},{6,14},{7,15},{8,0},{9,1},... | collective-permute-start | bytes 1572872 | tf_op jit(solution)/shard_map/ppermute | solution.py:151
  416.5 18.5 %collective-permute-start.56 = (bf16[8,128,256]{2,1,0:T(8,128)(2,1)S(1)}, bf16[8,128,256]{2,1,0:T(8,128)(2,1)S(1)}, u32[]{:S(2)}, u32[]{:S(2)}) collective-permute-start(bf16[8,128,256]{2,1,0:T(8,128)(2,1)S(1)} %collective-permute-done.54.refs_8_), channel_id=1, source_target_pairs={{0,2},{1,3},{2,0},{3,1},{4,6},{5,7},{6,4},{7,5},{8,10},{9,11},{10,... | collective-permute-start | bytes 1572872 | tf_op jit(solution)/shard_map/ppermute | solution.py:151
  416.5 18.5 %collective-permute-start.53 = (bf16[8,128,256]{2,1,0:T(8,128)(2,1)S(1)}, bf16[8,128,256]{2,1,0:T(8,128)(2,1)}, u32[]{:S(2)}, u32[]{:S(2)}) collective-permute-start(bf16[8,128,256]{2,1,0:T(8,128)(2,1)S(1)} %collective-permute-done.51.refs_5_), channel_id=1, source_target_pairs={{0,2},{1,3},{2,0},{3,1},{4,6},{5,7},{6,4},{7,5},{8,10},{9,11},{10,... | collective-permute-start | bytes 1572872 | tf_op jit(solution)/shard_map/ppermute | solution.py:151
  417.0 18.0 %collective-permute-start.57 = (bf16[8,128,256]{2,1,0:T(8,128)(2,1)S(1)}, bf16[8,128,256]{2,1,0:T(8,128)(2,1)}, u32[]{:S(2)}, u32[]{:S(2)}) collective-permute-start(bf16[8,128,256]{2,1,0:T(8,128)(2,1)S(1)} %collective-permute-done.55.refs_9_), channel_id=1, source_target_pairs={{0,2},{1,3},{2,0},{3,1},{4,6},{5,7},{6,4},{7,5},{8,10},{9,11},{10,... | collective-permute-start | bytes 1572872 | tf_op jit(solution)/shard_map/ppermute | solution.py:151
  417.1 17.9 %collective-permute-start.60 = (bf16[8,128,256]{2,1,0:T(8,128)(2,1)S(1)}, bf16[8,128,256]{2,1,0:T(8,128)(2,1)}, u32[]{:S(2)}, u32[]{:S(2)}) collective-permute-start(bf16[8,128,256]{2,1,0:T(8,128)(2,1)S(1)} %collective-permute-done.58.refs_12_), channel_id=1, source_target_pairs={{0,2},{1,3},{2,0},{3,1},{4,6},{5,7},{6,4},{7,5},{8,10},{9,11},{10,... | collective-permute-start | bytes 1572872 | tf_op jit(solution)/shard_map/ppermute | solution.py:151
  (73 other events, 1530.0 us)
where the time goes:
time: 490 us; the launch traced here: 489 us
  waiting for transfers between devices  230 us (47%)
  starting transfers between devices  147 us (30%)
  Pallas kernels  81.1 us (17%)
  local copies, waits for them, and re-layouts  17 us (3%)
  other arithmetic  13.1 us (3%)
    ppermute x79, waiting for transfers between devices, swapped(): return lax.ppermute(value, AXES, pairs)  230 us
    ppermute x79, starting transfers between devices, swapped(): return lax.ppermute(value, AXES, pairs)  142 us
    pallas_call x1, Pallas kernels, split_body(): run(functools.partial(attend_kernel, n, reach, heads), [context_shape, co...  41.2 us
    pallas_call x1, Pallas kernels, split_body(): run(functools.partial(key_kernel, n, reach), [jax.ShapeDtypeStruct((n, to...  19.2 us
    pallas_call x1, Pallas kernels, split_body(): run(functools.partial(output_kernel, n), [jax.ShapeDtypeStruct((part, out...  16.8 us
  transfers between devices with their start and end apart: 80, of which 38 were waited for; matrix products, arithmetic and copies ran while one was open for 4% of the time, Pallas kernels for 13%

commit v1 on v0

--- a/solution.py
+++ b/solution.py
@@ -6,6 +6,7 @@
 from jax import lax
 from jax.experimental import pallas as pl
 from jax.experimental.pallas import tpu as pltpu
+from jax.sharding import Mesh
 from jax.sharding import PartitionSpec as P
 
 
@@ -13,7 +14,6 @@
 WINDOW = 1024
 QUERY_SCALAR = 168
 VMEM_BYTES = 67_000_000
-AXES = ("rows", "cols", "sub")
 ANY = pl.BlockSpec(memory_space=pl.ANY)
 VMEM = pl.BlockSpec(memory_space=pltpu.VMEM)
 SMEM = pl.BlockSpec(memory_space=pltpu.SMEM)
@@ -144,11 +144,11 @@
 
 
 def swapped(value, place=0, col=0):
-    rows, cols = lax.axis_size("rows"), lax.axis_size("cols")
+    places, cols = lax.axis_size("place"), lax.axis_size("cols")
     pairs = [
-        (r * cols + c, (r ^ place) * cols + (c ^ col)) for r in range(rows) for c in range(cols)
+        (r * cols + c, (r ^ place) * cols + (c ^ col)) for r in range(places) for c in range(cols)
     ]
-    return lax.ppermute(value, AXES, pairs)
+    return lax.ppermute(value, ("place", "cols"), pairs)
 
 
 def run(kernel, out_shape, in_specs, out_specs, scratch, flops, bytes_moved):
@@ -165,32 +165,37 @@
     )
 
 
-def cut_kernel(n, meta, wq, wk, wv, *outs):
+def cut_kernel(n, meta, wq, wk, wv, kv_out, *q_outs):
     place = meta[0]
     wide_q = wq.shape[1] // n
-    wide_k = wk.shape[1] // n
+    for p in range(n):
+        kv_out[:, p * 2 * HD : p * 2 * HD + HD] = wk[:, p * HD : (p + 1) * HD]
+        kv_out[:, p * 2 * HD + HD : (p + 1) * 2 * HD] = wv[:, p * HD : (p + 1) * HD]
     for m in range(n):
         at = lax.bitwise_xor(place, m)
-        cols_k = pl.ds(pl.multiple_of(at * wide_k, 128), wide_k)
-        cols_q = pl.ds(pl.multiple_of(at * wide_q, 128), wide_q)
-        outs[m][:, :wide_k] = wk[:, cols_k]
-        outs[m][:, wide_k:] = wv[:, cols_k]
-        outs[n + m][...] = wq[:, cols_q]
-
-
-def load_all(n, meta, blocks, weights, block_mem, weight_mem, block_sem, weight_sem):
-    place, half = meta[0], meta[1]
-    deep = weights[0].shape[0]
+        q_outs[m][...] = wq[:, pl.ds(pl.multiple_of(at * wide_q, 128), wide_q)]
+
+
+def join_kernel(*refs):
+    out = refs[-1]
+    deep = refs[0].shape[0]
+    for m, piece in enumerate(refs[:-1]):
+        out[m * deep : (m + 1) * deep] = piece[...]
+
+
+def load_all(n, meta, blocks, weight_parts, block_mem, weight_mem, block_sem, weight_sem):
+    place = meta[0]
     copies = []
     for m in range(n):
-        for far in range(2):
+        for half in range(2):
+            source = weight_parts(m, half)
+            deep = source.shape[0]
             owner = lax.bitwise_xor(place, m)
-            rows = pl.ds(pl.multiple_of(owner * deep, 16), deep)
             copies.append(
                 pltpu.make_async_copy(
-                    weights[m * 2 + far],
-                    weight_mem.at[lax.bitwise_xor(half, far), rows, :],
-                    weight_sem.at[m * 2 + far],
+                    source,
+                    weight_mem.at[half, pl.ds(pl.multiple_of(owner * deep, 16), deep), :],
+                    weight_sem.at[m * 2 + half],
                 )
             )
     for copy in copies:
@@ -198,19 +203,23 @@
     for m in range(n):
         for side in range(2):
             pltpu.make_async_copy(
-                blocks[m * 2 + side], block_mem.at[m, side], block_sem.at[m, side]
+                blocks[m * 2 + side], block_mem.at[side, m], block_sem.at[m, side]
             ).start()
     return copies
 
 
-def project(m, meta, blocks, block_mem, weight_mem, block_sem):
+def project(t, meta, blocks, block_mem, weight_mem, block_sem):
     col = meta[2]
-    for side in range(2):
-        pltpu.make_async_copy(blocks[side], block_mem.at[m, side], block_sem.at[m, side]).wait()
-    return jnp.dot(
-        block_mem[m, 0], weight_mem[col], preferred_element_type=jnp.float32
-    ) + jnp.dot(
-        block_mem[m, 1], weight_mem[lax.bitwise_xor(col, 1)], preferred_element_type=jnp.float32
+    _, _, tokens, features = block_mem.shape
+    for m in range(2):
+        for side in range(2):
+            pltpu.make_async_copy(
+                blocks[side], block_mem.at[side, 2 * t + m], block_sem.at[2 * t + m, side]
+            ).wait()
+    same = block_mem[0, pl.ds(2 * t, 2)].reshape(2 * tokens, features)
+    other = block_mem[1, pl.ds(2 * t, 2)].reshape(2 * tokens, features)
+    return jnp.dot(same, weight_mem[col], preferred_element_type=jnp.float32) + jnp.dot(
+        other, weight_mem[lax.bitwise_xor(col, 1)], preferred_element_type=jnp.float32
     )
 
 
@@ -220,36 +229,51 @@
 
 
 def key_kernel(n, reach, meta, cosine, sine, gain, *refs):
-    blocks, weights = refs[: 2 * n], refs[2 * n : 4 * n]
-    kv_out, tail_out, block_mem, weight_mem, block_sem, weight_sem = refs[4 * n :]
-    copies = load_all(n, meta, blocks, weights, block_mem, weight_mem, block_sem, weight_sem)
+    blocks, weights = refs[: 2 * n], refs[2 * n : 3 * n]
+    kv_out, tail_out, block_mem, weight_mem, block_sem, weight_sem = refs[3 * n :]
+    deep = weights[0].shape[0] // 2
+
+    def part(m, half):
+        return weights[m].at[pl.ds(half * deep, deep)]
+
+    copies = load_all(n, meta, blocks, part, block_mem, weight_mem, block_sem, weight_sem)
     for copy in copies:
         copy.wait()
     place = meta[0]
-
-    @pl.loop(0, n)
-    def _(m):
-        at = lax.bitwise_xor(place, m)
-        raw = project(m, meta, blocks, block_mem, weight_mem, block_sem)
-        keys = normed_rotated(raw[:, :HD], gain[...], cosine[at], sine[at]).astype(jnp.bfloat16)
-        values = raw[:, HD:].astype(jnp.bfloat16)
-        kv_out[m, :, :HD] = keys
-        kv_out[m, :, HD:] = values
-
-        @pl.when(at >= n - reach)
-        def _():
-            tail_out[at - (n - reach), :, :HD] = keys
-            tail_out[at - (n - reach), :, HD:] = values
+    tokens = block_mem.shape[2]
+
+    @pl.loop(0, n // 2)
+    def _(t):
+        raw_two = project(t, meta, blocks, block_mem, weight_mem, block_sem)
+        for m in range(2):
+            slot = 2 * t + m
+            at = lax.bitwise_xor(place, slot)
+            raw = raw_two[m * tokens : (m + 1) * tokens]
+            keys = normed_rotated(raw[:, :HD], gain[...], cosine[at], sine[at])
+            keys = keys.astype(jnp.bfloat16)
+            values = raw[:, HD:].astype(jnp.bfloat16)
+            kv_out[slot, :, :HD] = keys
+            kv_out[slot, :, HD:] = values
+
+            @pl.when(at >= n - reach)
+            def _():
+                tail_out[at - (n - reach), :, :HD] = keys
+                tail_out[at - (n - reach), :, HD:] = values
 
 
 def attend_kernel(n, reach, heads, meta, cosine, sine, gain, q_doc, k_doc, kv_own, kv_back, *refs):
-    blocks, weights = refs[: 2 * n], refs[2 * n : 4 * n]
-    keep_out, send_out = refs[4 * n : 4 * n + 2]
-    block_mem, weight_mem, kv_mem, block_sem, weight_sem, kv_sem = refs[4 * n + 2 :]
+    blocks, weight = refs[: 2 * n], refs[2 * n]
+    keep_out, send_out = refs[2 * n + 1 : 2 * n + 3]
+    block_mem, weight_mem, kv_mem, block_sem, weight_sem, kv_sem = refs[2 * n + 3 :]
     place, col = meta[0], meta[2]
     tokens = block_mem.shape[2]
     part = tokens // 2
-    copies = load_all(n, meta, blocks, weights, block_mem, weight_mem, block_sem, weight_sem)
+    deep = weight.shape[0] // (2 * n)
+
+    def rows(m, half):
+        return weight.at[pl.ds((half * n + m) * deep, deep)]
+
+    copies = load_all(n, meta, blocks, rows, block_mem, weight_mem, block_sem, weight_sem)
     more = [pltpu.make_async_copy(kv_back, kv_mem.at[pl.ds(0, reach)], kv_sem.at[n])]
     for m in range(n):
         more.append(
@@ -265,65 +289,73 @@
     row_at = lax.broadcasted_iota(jnp.int32, (tokens, tokens), 0)
     col_at = lax.broadcasted_iota(jnp.int32, (tokens, tokens), 1)
 
-    @pl.loop(0, n)
-    def _(m):
-        at = lax.bitwise_xor(place, m)
-        raw = project(m, meta, blocks, block_mem, weight_mem, block_sem)
-        cosine_here, sine_here = cosine[at], sine[at]
-        queries = [
-            normed_rotated(
-                raw[:, h * HD : (h + 1) * HD], gain[...], cosine_here, sine_here
-            ).astype(jnp.bfloat16)
-            for h in range(heads)
-        ]
-        doc = q_doc[at]
-        totals = [jnp.zeros((tokens, 1), jnp.float32) for _ in range(heads)]
-        mixed = [jnp.zeros((tokens, HD), jnp.float32) for _ in range(heads)]
-        for step in range(reach + 1):
-            pair = kv_mem[at + step]
-            visible = doc == k_doc[at + step]
-            if step == 0:
-                visible = visible & (row_at < col_at)
-            if step == reach:
-                visible = visible & (row_at >= col_at)
-            for h in range(heads):
+    @pl.loop(0, n // 2)
+    def _(t):
+        raw_two = project(t, meta, blocks, block_mem, weight_mem, block_sem)
+        for m in range(2):
+            at = lax.bitwise_xor(place, 2 * t + m)
+            raw = raw_two[m * tokens : (m + 1) * tokens]
+            cosine_here, sine_here = cosine[at], sine[at]
+            queries = jnp.concatenate(
+                [
+                    normed_rotated(
+                        raw[:, h * HD : (h + 1) * HD], gain[...], cosine_here, sine_here
+                    ).astype(jnp.bfloat16)
+                    for h in range(heads)
+                ],
+                axis=0,
+            )
+            doc = q_doc[at]
+            totals = jnp.zeros((heads * tokens, 1), jnp.float32)
+            mixed = jnp.zeros((heads * tokens, HD), jnp.float32)
+            for step in range(reach + 1):
+                pair = kv_mem[at + step]
+                visible = doc == k_doc[at + step]
+                if step == 0:
+                    visible = visible & (row_at < col_at)
+                if step == reach:
+                    visible = visible & (row_at >= col_at)
                 scores = lax.dot_general(
-                    queries[h],
+                    queries,
                     pair[:, :HD],
                     (((1,), (1,)), ((), ())),
                     preferred_element_type=jnp.float32,
                 )
-                weights_here = jnp.where(visible, jnp.exp(scores * scale), 0.0)
-                totals[h] = totals[h] + jnp.sum(weights_here, axis=-1, keepdims=True)
-                mixed[h] = mixed[h] + jnp.dot(
+                weights_here = jnp.where(
+                    visible[None],
+                    jnp.exp(scores * scale).reshape(heads, tokens, tokens),
+                    0.0,
+                ).reshape(heads * tokens, tokens)
+                totals = totals + jnp.sum(weights_here, axis=-1, keepdims=True)
+                mixed = mixed + jnp.dot(
                     weights_here.astype(jnp.bfloat16),
                     pair[:, HD:],
                     preferred_element_type=jnp.float32,
                 )
-        for h in range(heads):
-            done = (mixed[h] / totals[h]).astype(jnp.bfloat16)
-            top, bottom = done[:part], done[part:]
-            keep_out[at, :, h * HD : (h + 1) * HD] = jnp.where(col == 0, top, bottom)
-            send_out[at, :, h * HD : (h + 1) * HD] = jnp.where(col == 0, bottom, top)
+            done = (mixed / totals).astype(jnp.bfloat16)
+            for h in range(heads):
+                top = done[h * tokens : h * tokens + part]
+                bottom = done[h * tokens + part : (h + 1) * tokens]
+                keep_out[at, :, h * HD : (h + 1) * HD] = jnp.where(col == 0, top, bottom)
+                send_out[at, :, h * HD : (h + 1) * HD] = jnp.where(col == 0, bottom, top)
 
 
 def output_kernel(n, meta, *refs):
-    contexts, weights = refs[: 2 * n], refs[2 * n : 2 * n + 4]
-    outs = refs[2 * n + 4 : 4 * n + 4]
-    context_mem, weight_mem, result_mem, context_sem, weight_sem = refs[4 * n + 4 :]
-    place, half, col = meta[0], meta[1], meta[2]
-    deep = weights[0].shape[0]
+    contexts, weights = refs[: 2 * n], refs[2 * n]
+    outs = refs[2 * n + 1 : 4 * n + 1]
+    context_mem, weight_mem, result_mem, context_sem, weight_sem = refs[4 * n + 1 :]
+    place, col = meta[0], meta[2]
+    deep = weights.shape[2]
     wide = contexts[0].shape[2]
     part = contexts[0].shape[1]
     copies = []
-    for far in range(2):
+    for half in range(2):
         for side in range(2):
-            rows = pl.ds(pl.multiple_of(lax.bitwise_xor(col, side) * deep, 16), deep)
             copies.append(
                 pltpu.make_async_copy(
-                    weights[far * 2 + side],
-                    weight_mem.at[lax.bitwise_xor(half, far), rows, :],
-                    weight_sem.at[far * 2 + side],
+                    weights.at[half, side],
+                    weight_mem.at[half, pl.ds(side * deep, deep), :],
+                    weight_sem.at[half * 2 + side],
                 )
             )
     for m in range(n):
@@ -341,12 +373,12 @@
     for copy in copies:
         copy.wait()
 
-    @pl.loop(0, n // 2)
+    @pl.loop(0, n // 4)
     def _(t):
-        left = context_mem[pl.ds(2 * t, 2)].reshape(2 * part, 2 * deep)
+        left = context_mem[pl.ds(4 * t, 4)].reshape(4 * part, 2 * deep)
         for block in range(2):
             result = jnp.dot(left, weight_mem[block], preferred_element_type=jnp.float32)
-            result_mem[block, pl.ds(2 * t, 2)] = result.astype(jnp.bfloat16).reshape(2, part, -1)
+            result_mem[block, pl.ds(4 * t, 4)] = result.astype(jnp.bfloat16).reshape(4, part, -1)
 
     for m in range(n):
         for side in range(2):
@@ -371,23 +403,22 @@
     heads = query_weight.shape[1] // key_weight.shape[1]
     reach = WINDOW // tokens
     part = tokens // 2
-    row = lax.axis_index("rows")
-    col = lax.axis_index("cols")
-    half, place = row // n, row % n
+    half, place, col = lax.axis_index("half"), lax.axis_index("place"), lax.axis_index("cols")
     meta = jnp.stack([place, half, col]).astype(jnp.int32)
     bf16, f32 = jnp.bfloat16, jnp.float32
 
     deep = query_weight.shape[0]
-    pieces = run(
+    kv_cut, *q_cut = run(
         functools.partial(cut_kernel, n),
-        [jax.ShapeDtypeStruct((deep, 2 * HD), bf16)] * n
+        [jax.ShapeDtypeStruct((deep, n * 2 * HD), bf16)]
         + [jax.ShapeDtypeStruct((deep, heads * HD), bf16)] * n,
         [SMEM, VMEM, VMEM, VMEM],
-        [VMEM] * (2 * n),
+        [VMEM] * (n + 1),
         [],
         0,
         4 * query_weight.size * 2,
     )(meta, query_weight, key_weight, value_weight)
+    kv_rows = lax.all_gather(kv_cut, "half", axis=0, tiled=True)
 
     wide = activations.astype(f32)
     squares = jnp.sum(wide * wide, axis=-1).reshape(2, part)
@@ -398,26 +429,33 @@
 
     z, y, c = n // 2, n // 4, 1
     blocks = {(0, 0): normed}
-    blocks[z, 0] = swapped(normed, z, 0)
     blocks[y, 0] = swapped(normed, y, 0)
     blocks[0, 1] = swapped(normed, 0, 1)
+    blocks[z, 0] = swapped(normed, z, 0)
+    blocks[y, 1] = swapped(blocks[y, 0], 0, 1)
+    blocks[z, 1] = swapped(blocks[z, 0], 0, 1)
     blocks[z + y, 0] = swapped(blocks[z, 0], y, 0)
-    blocks[z, 1] = swapped(blocks[z, 0], 0, 1)
-    blocks[y, 1] = swapped(blocks[y, 0], 0, 1)
-    blocks[z + y, 1] = swapped(blocks[z, 1], y, 0)
+    blocks[z + y, 1] = swapped(blocks[z + y, 0], 0, 1)
     for m, side in list(blocks):
         blocks[m + c, side] = swapped(blocks[m, side], c, 0)
     block_list = [blocks[m, side] for m in range(n) for side in range(2)]
 
-    def spread(mine):
-        out = []
-        for m in range(n):
-            piece = mine[m] if m == 0 else swapped(mine[m], m, 0)
-            out += [piece, swapped(piece, n, 0)]
-        return out
-
-    kv_weights = spread(pieces[:n])
-    q_weights = spread(pieces[n:])
+    q_pieces = [q_cut[0]] + [swapped(q_cut[m], m, 0) for m in range(1, n)]
+    q_own = run(
+        join_kernel,
+        jax.ShapeDtypeStruct((n * deep, heads * HD), bf16),
+        [VMEM] * n,
+        VMEM,
+        [],
+        0,
+        4 * q_cut[0].size * n,
+    )(*q_pieces)
+    q_weight = lax.all_gather(q_own, "half", axis=0, tiled=True)
+    kv_weights = []
+    for m in range(n):
+        first = lax.bitwise_xor(place, m) * 2 * HD
+        piece = lax.dynamic_slice_in_dim(kv_rows, first, 2 * HD, 1)
+        kv_weights.append(piece if m == 0 else swapped(piece, m, 0))
 
     in_half = lax.dynamic_slice_in_dim(positions, half * n * tokens, n * tokens, 0)
     frequency = 10000.0 ** (-(jnp.arange(HD // 2, dtype=f32) * 2.0 / HD))
@@ -435,7 +473,7 @@
 
     block_bytes = 2 * n * tokens * features * 2
     stores = [
-        pltpu.VMEM((n, 2, tokens, features), bf16),
+        pltpu.VMEM((2, n, tokens, features), bf16),
         pltpu.VMEM((2, features, 2 * HD), bf16),
     ]
     sems = [pltpu.SemaphoreType.DMA((n, 2)), pltpu.SemaphoreType.DMA((2 * n,))]
@@ -446,19 +484,19 @@
             jax.ShapeDtypeStruct((n, tokens, 2 * HD), bf16),
             jax.ShapeDtypeStruct((reach, tokens, 2 * HD), bf16),
         ],
-        [SMEM, VMEM, VMEM, VMEM] + [ANY] * (4 * n),
+        [SMEM, VMEM, VMEM, VMEM] + [ANY] * (3 * n),
         [VMEM, VMEM],
         stores + sems,
         flops,
         block_bytes,
     )(meta, cosine, sine, key_gain.reshape(1, HD), *block_list, *kv_weights)
-    kv_back = passed_along(kv_tail, "rows", n)
+    kv_back = lax.ppermute(kv_tail, "half", [(0, 1)])
 
     context_shape = jax.ShapeDtypeStruct((n, part, heads * HD), bf16)
     keep, send = run(
         functools.partial(attend_kernel, n, reach, heads),
         [context_shape, context_shape],
-        [SMEM, VMEM, VMEM, VMEM, VMEM, VMEM, ANY, ANY] + [ANY] * (4 * n),
+        [SMEM, VMEM, VMEM, VMEM, VMEM, VMEM, ANY, ANY] + [ANY] * (2 * n + 1),
         [VMEM, VMEM],
         stores
         + [pltpu.VMEM((n + reach, tokens, 2 * HD), bf16)]
@@ -476,11 +514,12 @@
         kv_own,
         kv_back,
         *block_list,
-        *q_weights,
-    )
-
-    out_far = swapped(output_weight, n, 0)
-    out_weights = [output_weight, swapped(output_weight, 0, 1), out_far, swapped(out_far, 0, 1)]
+        q_weight,
+    )
+
+    own_weight, _ = lax.optimization_barrier((output_weight, q_own))
+    out_weights = lax.all_gather(own_weight, ("half", "cols"), axis=0)
+    out_weights = out_weights.reshape(2, 2, *output_weight.shape)
 
     there = swapped(send, 0, 1)
     contexts = {(0, 0): keep, (0, 1): there}
@@ -499,7 +538,7 @@
     results = run(
         functools.partial(output_kernel, n),
         [jax.ShapeDtypeStruct((part, out_cols), bf16)] * (2 * n),
-        [SMEM] + [ANY] * (2 * n + 4),
+        [SMEM] + [ANY] * (2 * n + 1),
         [VMEM] * (2 * n),
         [
             pltpu.VMEM((n, part, 2 * deep_out), bf16),
@@ -510,7 +549,7 @@
         ],
         2 * n * part * 2 * deep_out * 2 * out_cols,
         16 * deep_out * out_cols,
-    )(meta, *context_list, *out_weights)
+    )(meta, *context_list, out_weights)
 
     arrived = [
         [
@@ -536,49 +575,33 @@
     return (wide + summed.astype(f32)).astype(bf16)
 
 
-def fits(mesh, activations, key_weight):
-    rows = mesh.shape["rows"]
-    tokens = activations.shape[0] // (mesh.shape["groups"] * rows)
-    splits = mesh.shape["cols"] * mesh.shape["sub"]
-    n = key_weight.shape[1] // HD // splits
-    return (
-        mesh.shape["cols"] == 2
-        and mesh.shape["sub"] == 1
-        and n == 8
-        and rows == 2 * n
-        and WINDOW % tokens == 0
-        and WINDOW // tokens <= n
-        and tokens % 256 == 0
-    )
-
-
 def solution(mesh):
+    sizes = mesh.shape
+    if sizes["cols"] == 2 and sizes["sub"] == 1 and sizes["rows"] == 16:
+        shape = (sizes["groups"], 2, sizes["rows"] // 2, sizes["cols"], sizes["sub"])
+        names = ("groups", "half", "place", "cols", "sub")
+        fine, rows = Mesh(mesh.devices.reshape(shape), names), ("half", "place")
+    else:
+        fine, rows = mesh, ("rows",)
+    columns = ("cols", "sub")
     placed = (
-        P(("groups", "rows"), ("cols", "sub")),
+        P(("groups", *rows), columns),
         P("groups"),
-        P("rows", ("cols", "sub")),
-        P("rows", ("cols", "sub")),
-        P("rows", ("cols", "sub")),
-        P(("cols", "sub"), "rows"),
+        P(rows, columns),
+        P(rows, columns),
+        P(rows, columns),
+        P(columns, rows),
         P(),
         P(),
         P(),
     )
 
-    def step(activations, positions, query_weight, key_weight, *rest):
-        whole = not fits(mesh, activations, key_weight)
-
-        def body(*args):
-            if whole:
-                return gathered_body(*args)
-            return split_body(*args)
-
+    def mapped(body):
         return jax.shard_map(
-            body,
-            mesh=mesh,
-            in_specs=placed,
-            out_specs=P(("groups", "rows"), ("cols", "sub")),
-            check_vma=False,
-        )(activations, positions, query_weight, key_weight, *rest)
-
-    return step
+            body, mesh=fine, in_specs=placed, out_specs=placed[0], check_vma=False
+        )
+
+    if fine is mesh:
+        return mapped(gathered_body)
+
+    return mapped(split_body)

time: 490 us -> 465 us (0.949)
  starting transfers between devices: 147 us -> 72.1 us
  waiting for transfers between devices: 230 us -> 272 us
  between operations: 0.53 us -> 13.6 us
    ppermute x80 -> x61, starting transfers between devices: 147 us -> 72.1 us  [the longest x60 70 us: swapped(): return lax.ppermute(value, ('place', 'cols'), pairs)]
    ppermute x80 -> x61, waiting for transfers between devices: 230 us -> 272 us  [the longest x60 263 us: swapped(): return lax.ppermute(value, ('place', 'cols'), pairs)]
    all_gather x0 -> x1, local copies, waits for them, and re-layouts: none -> 8.26 us  [split_body(): out_weights = lax.all_gather(own_weight, ('half', 'cols'), axis=0)]
    ppermute x3 -> x0, local copies, waits for them, and re-layouts: 7.7 us -> none  [swapped(): return lax.ppermute(value, AXES, pairs)]
    pallas_call x1, Pallas kernels: 41.2 us -> 35 us  [split_body(): run(functools.partial(attend_kernel, n, reach, heads), [context_shape, co...]
  transfers between devices with their start and end apart: 80 -> 64, of which waited for: 38 -> 31; matrix products, arithmetic and copies ran while one was open for 4% -> 5% of each run, Pallas kernels for 13% -> 12%
where the time goes in v1:
time: 465 us; the launch traced here: 464 us
  waiting for transfers between devices  272 us (58%)
  Pallas kernels  76.3 us (16%)
  starting transfers between devices  72.1 us (16%)
  local copies, waits for them, and re-layouts  20.5 us (4%)
  between operations  13.6 us (3%)
  other arithmetic  9.76 us (2%)
    ppermute x60, waiting for transfers between devices, swapped(): return lax.ppermute(value, ('place', 'cols'), pairs)  263 us
    ppermute x60, starting transfers between devices, swapped(): return lax.ppermute(value, ('place', 'cols'), pairs)  70 us
    pallas_call x1, Pallas kernels, split_body(): run(functools.partial(attend_kernel, n, reach, heads), [context_shape, co...  35 us
    pallas_call x1, Pallas kernels, split_body(): run(functools.partial(key_kernel, n, reach), [jax.ShapeDtypeStruct((n, to...  18.6 us
    pallas_call x1, Pallas kernels, split_body(): run(functools.partial(output_kernel, n), [jax.ShapeDtypeStruct((part, out...  16.3 us
  transfers between devices with their start and end apart: 64, of which 31 were waited for; matrix products, arithmetic and copies ran while one was open for 5% of the time, Pallas kernels for 12%

profile of v1, /device:TPU:0, one launch (start us, length us, event | category | flops | bytes accessed | tf_op | source)
XLA Modules:
  0.0 464.2 jit_solution(860462301988546754)
XLA Ops:
  7.2 3.7 shard_map.91
  12.3 2.6 collective-permute-start.25
  15.0 1.7 collective-permute-start.27
  16.8 2.6 collective-permute-start.29
  20.2 1.7 collective-permute-start.30
  21.9 1.5 collective-permute-done.26.refs_3_
  23.4 4.5 collective-permute-done.28.refs_5_
  27.9 8.2 %collective-permute-done.29.refs_6_ = bf16[336,256]{1,0:T(8,128)(2,1)} collective-permute-done((bf16[336,256]{1,0:T(8,128)(2,1)S(1)}, bf16[336,256]{1,0:T(8,128)(2,1)}, u32[]{:S(2)}, u32[]{:S(2)}) %collective-permute-start.29) | collective-permute-done | bytes 172064 | tf_op jit(solution)/shard_map/ppermute | solution.py:151
  36.1 6.0 %collective-permute-done.30.refs_7_ = bf16[336,256]{1,0:T(8,128)(2,1)} collective-permute-done((bf16[336,256]{1,0:T(8,128)(2,1)S(1)}, bf16[336,256]{1,0:T(8,128)(2,1)}, u32[]{:S(2)}, u32[]{:S(2)}) %collective-permute-start.30) | collective-permute-done | bytes 172064 | tf_op jit(solution)/shard_map/ppermute | solution.py:151
  42.0 2.6 shard_map.93
  47.7 2.2 collective-permute-done
  50.4 1.6 collective-permute-start.8
  54.3 50.4 %collective-permute-done.8.refs_8_ = bf16[256,2688]{1,0:T(8,128)(2,1)S(1)} collective-permute-done((bf16[256,2688]{1,0:T(8,128)(2,1)S(1)}, bf16[256,2688]{1,0:T(8,128)(2,1)S(1)}, u32[]{:S(2)}, u32[]{:S(2)}) %collective-permute-start.8) | collective-permute-done | bytes 1376288 | tf_op jit(solution)/shard_map/ppermute | solution.py:151
  108.0 29.1 %collective-permute-done.12.refs_12_ = bf16[256,2688]{1,0:T(8,128)(2,1)} collective-permute-done((bf16[256,2688]{1,0:T(8,128)(2,1)S(1)}, bf16[256,2688]{1,0:T(8,128)(2,1)}, u32[]{:S(2)}, u32[]{:S(2)}) %collective-permute-start.12) | collective-permute-done | bytes 1376288 | tf_op jit(solution)/shard_map/ppermute | solution.py:151
  137.1 1.4 collective-permute-done.9.refs_9_
  139.7 2.7 constant_dynamic-slice_fusion
  142.4 25.6 %collective-permute-done.5.refs_5_ = bf16[256,2688]{1,0:T(8,128)(2,1)} collective-permute-done((bf16[256,2688]{1,0:T(8,128)(2,1)}, bf16[256,2688]{1,0:T(8,128)(2,1)}, u32[]{:S(2)}, u32[]{:S(2)}) %collective-permute-start.5) | collective-permute-done | bytes 1376288 | tf_op jit(solution)/shard_map/ppermute | solution.py:151
  168.0 1.4 collective-permute-start.17
  170.2 8.7 %collective-permute-done.17.refs_18_ = bf16[672,256]{1,0:T(8,128)(2,1)S(1)} collective-permute-done((bf16[672,256]{1,0:T(8,128)(2,1)S(1)}, bf16[672,256]{1,0:T(8,128)(2,1)S(1)}, u32[]{:S(2)}, u32[]{:S(2)}) %collective-permute-start.17) | collective-permute-done | bytes 344096 | tf_op jit(solution)/shard_map/ppermute | solution.py:151
  178.9 6.4 %collective-permute-done.18.refs_19_ = bf16[672,256]{1,0:T(8,128)(2,1)S(1)} collective-permute-done((bf16[672,256]{1,0:T(8,128)(2,1)S(1)}, bf16[672,256]{1,0:T(8,128)(2,1)S(1)}, u32[]{:S(2)}, u32[]{:S(2)}) %collective-permute-start.18) | collective-permute-done | bytes 344096 | tf_op jit(solution)/shard_map/ppermute | solution.py:151
  186.1 31.3 %collective-permute-done.13.refs_13_ = bf16[256,2688]{1,0:T(8,128)(2,1)} collective-permute-done((bf16[256,2688]{1,0:T(8,128)(2,1)}, bf16[256,2688]{1,0:T(8,128)(2,1)}, u32[]{:S(2)}, u32[]{:S(2)}) %collective-permute-start.13) | collective-permute-done | bytes 1376288 | tf_op jit(solution)/shard_map/ppermute | solution.py:151
  217.5 16.7 %collective-permute-done.20.refs_21_ = bf16[672,256]{1,0:T(8,128)(2,1)S(1)} collective-permute-done((bf16[672,256]{1,0:T(8,128)(2,1)S(1)}, bf16[672,256]{1,0:T(8,128)(2,1)S(1)}, u32[]{:S(2)}, u32[]{:S(2)}) %collective-permute-start.20) | collective-permute-done | bytes 344096 | tf_op jit(solution)/shard_map/ppermute | solution.py:151
  235.0 2.4 collective-permute-start.21
  237.5 29.9 %collective-permute-done.21.refs_22_ = bf16[672,256]{1,0:T(8,128)(2,1)S(1)} collective-permute-done((bf16[672,256]{1,0:T(8,128)(2,1)S(1)}, bf16[672,256]{1,0:T(8,128)(2,1)S(1)}, u32[]{:S(2)}, u32[]{:S(2)}) %collective-permute-start.21) | collective-permute-done | bytes 344096 | tf_op jit(solution)/shard_map/ppermute | solution.py:151
  267.4 3.7 fusion.4
  272.4 1.3 pad_maximum_fusion.1.sine
  273.8 4.8 %collective-permute-done.22.refs_23_ = bf16[672,256]{1,0:T(8,128)(2,1)S(1)} collective-permute-done((bf16[672,256]{1,0:T(8,128)(2,1)S(1)}, bf16[672,256]{1,0:T(8,128)(2,1)S(1)}, u32[]{:S(2)}, u32[]{:S(2)}) %collective-permute-start.22) | collective-permute-done | bytes 344096 | tf_op jit(solution)/shard_map/ppermute | solution.py:151
  279.3 18.6 %shard_map.92 = (bf16[8,256,256]{2,1,0:T(8,128)(2,1)}, bf16[4,256,256]{2,1,0:T(8,128)(2,1)}) custom-call(s32[3]{0:T(128)} %pad_add_fusion.meta, f32[8,256,128]{2,1,0:T(8,128)} %pad_maximum_fusion.cosine, f32[8,256,128]{2,1,0:T(8,128)} %pad_maximum_fusion.1.sine, f32[1,128]{1,0:T(1,128)} %bitcast.14, bf16[256,2688]{1,0:T(8,128)(2,1)} %copy-done.2, ...), custom_call_target="tpu_custom_call" | custom-call | flops 5637144576 | bytes 22020096 | tf_op jit(solution)/shard_map/pallas_call | solution.py:481
  298.0 2.1 collective-permute-start.23
  300.1 1.9 slice.15.q_doc
  302.5 8.8 %collective-permute-done.23.kv_back = bf16[4,256,256]{2,1,0:T(8,128)(2,1)} collective-permute-done((bf16[4,256,256]{2,1,0:T(8,128)(2,1)}, bf16[4,256,256]{2,1,0:T(8,128)(2,1)}, u32[]{:S(2)}, u32[]{:S(2)}) %collective-permute-start.23) | collective-permute-done | bytes 524320 | tf_op jit(solution)/shard_map/ppermute | solution.py:493
  311.3 35.0 %shard_map.94 = (bf16[8,128,256]{2,1,0:T(8,128)(2,1)}, bf16[8,128,256]{2,1,0:T(8,128)(2,1)}) custom-call(s32[3]{0:T(128)} %pad_add_fusion.meta, f32[8,256,128]{2,1,0:T(8,128)} %pad_maximum_fusion.cosine, f32[8,256,128]{2,1,0:T(8,128)} %pad_maximum_fusion.1.sine, f32[1,128]{1,0:T(1,128)} %bitcast.15, s32[8,256,1]{2,1,0:T(8,128)} %slice.15.q_doc, ...), custom_call_target="tpu_custom_call" | custom-call | flops 11274289152 | bytes 22020096 | tf_op jit(solution)/shard_map/pallas_call | solution.py:496
  346.4 2.5 collective-permute-start.31
  348.9 12.7 %collective-permute-start.38 = (bf16[8,128,256]{2,1,0:T(8,128)(2,1)}, bf16[8,128,256]{2,1,0:T(8,128)(2,1)S(1)}, u32[]{:S(2)}, u32[]{:S(2)}) collective-permute-start(bf16[8,128,256]{2,1,0:T(8,128)(2,1)} %get-tuple-element.46.refs_0_), channel_id=1, source_target_pairs={{0,8},{1,9},{2,10},{3,11},{4,12},{5,13},{6,14},{7,15},{8,0},{9,1},... | collective-permute-start | bytes 1572872 | tf_op jit(solution)/shard_map/ppermute | solution.py:151
  361.5 1.5 collective-permute-start.34
  363.6 11.7 %collective-permute-start.39 = (bf16[8,128,256]{2,1,0:T(8,128)(2,1)S(1)}, bf16[8,128,256]{2,1,0:T(8,128)(2,1)S(1)}, u32[]{:S(2)}, u32[]{:S(2)}) collective-permute-start(bf16[8,128,256]{2,1,0:T(8,128)(2,1)S(1)} %collective-permute-done.31.refs_1_), channel_id=1, source_target_pairs={{0,8},{1,9},{2,10},{3,11},{4,12},{5,13},{6,14},{7,15},{8,0},{9,1},... | collective-permute-start | bytes 1572872 | tf_op jit(solution)/shard_map/ppermute | solution.py:151
  377.0 10.7 %collective-permute-done.35.refs_5_ = bf16[8,128,256]{2,1,0:T(8,128)(2,1)S(1)} collective-permute-done((bf16[8,128,256]{2,1,0:T(8,128)(2,1)S(1)}, bf16[8,128,256]{2,1,0:T(8,128)(2,1)S(1)}, u32[]{:S(2)}, u32[]{:S(2)}) %collective-permute-start.35) | collective-permute-done | bytes 524320 | tf_op jit(solution)/shard_map/ppermute | solution.py:151
  388.7 8.8 %collective-permute-done.42.refs_12_ = bf16[8,128,256]{2,1,0:T(8,128)(2,1)S(1)} collective-permute-done((bf16[8,128,256]{2,1,0:T(8,128)(2,1)S(1)}, bf16[8,128,256]{2,1,0:T(8,128)(2,1)S(1)}, u32[]{:S(2)}, u32[]{:S(2)}) %collective-permute-start.42) | collective-permute-done | bytes 524320 | tf_op jit(solution)/shard_map/ppermute | solution.py:151
  399.1 8.3 %copy.12 = bf16[8192,336]{1,0:T(8,128)(2,1)} copy(bf16[8192,336]{0,1:T(8,128)(2,1)} %all-gather.9.cloned.1.call-done) | data formatting | bytes 11010048 | tf_op jit(solution)/shard_map/all_gather | solution.py:521
  408.2 16.3 %shard_map.95 = (bf16[128,336]{1,0:T(8,128)(2,1)}, bf16[128,336]{1,0:T(8,128)(2,1)}, bf16[128,336]{1,0:T(8,128)(2,1)}, bf16[128,336]{1,0:T(8,128)(2,1)}, bf16[12...) custom-call(s32[3]{0:T(128)} %pad_add_fusion.meta, ...), custom_call_target="tpu_custom_call" | custom-call | flops 5637144576 | bytes 11010048 | tf_op jit(solution)/shard_map/pallas_call | solution.py:538
  424.6 2.7 collective-permute-start.53
  430.8 1.4 collective-permute-start.57
  432.2 1.4 collective-permute-start.58
  436.0 2.2 collective-permute-done.56
  438.3 2.2 collective-permute-done.57
  440.4 1.5 collective-permute-start.47
  451.7 2.4 collective-permute-done.51
  456.2 1.4 fusion.3
  (181 shorter events, 41.6 us)
Async XLA Ops:
  6.5 133.2 %all-gather.5.cloned.1.call-start = ((), (), s32[]{:S(2)}) async-start(), calls=%async_computation | async-start | bytes 4128768 | tf_op jit(solution)/shard_map/all_gather | solution.py:421
  11.0 291.6 %all-gather.7.cloned.1.call-start = ((), (), s32[]{:S(2)}) async-start(), calls=%async_computation.1 | async-start | bytes 4128768 | tf_op jit(solution)/shard_map/all_gather | solution.py:453
  16.7 11.2 %collective-permute-start.28 = (bf16[336,256]{1,0:T(8,128)(2,1)S(1)}, bf16[336,256]{1,0:T(8,128)(2,1)}, u32[]{:S(2)}, u32[]{:S(2)}) collective-permute-start(bf16[336,256]{1,0:T(8,128)(2,1)S(1)} %copy-done.27), channel_id=1, source_target_pairs={{0,10},{1,11},{2,8},{3,9},{4,14},{5,15},{6,12},{7,13},{8,2},{9,3},... | collective-permute-start | bytes 516104 | tf_op jit(solution)/shard_map/ppermute | solution.py:151
  16.8 19.3 %collective-permute-start.29 = (bf16[336,256]{1,0:T(8,128)(2,1)S(1)}, bf16[336,256]{1,0:T(8,128)(2,1)}, u32[]{:S(2)}, u32[]{:S(2)}) collective-permute-start(bf16[336,256]{1,0:T(8,128)(2,1)S(1)} %copy-done.26), channel_id=1, source_target_pairs={{0,12},{1,13},{2,14},{3,15},{4,8},{5,9},{6,10},{7,11},{8,4},{9,5},... | collective-permute-start | bytes 516104 | tf_op jit(solution)/shard_map/ppermute | solution.py:151
  20.2 21.8 %collective-permute-start.30 = (bf16[336,256]{1,0:T(8,128)(2,1)S(1)}, bf16[336,256]{1,0:T(8,128)(2,1)}, u32[]{:S(2)}, u32[]{:S(2)}) collective-permute-start(bf16[336,256]{1,0:T(8,128)(2,1)S(1)} %copy-done.25), channel_id=1, source_target_pairs={{0,14},{1,15},{2,12},{3,13},{4,10},{5,11},{6,8},{7,9},{8,6},{9,7},... | collective-permute-start | bytes 516104 | tf_op jit(solution)/shard_map/ppermute | solution.py:151
  44.7 354.4 %all-gather.9.cloned.1.call-start = ((), (), s32[]{:S(2)}) async-start(), calls=%async_computation.2 | async-start | bytes 6881280 | tf_op jit(solution)/shard_map/all_gather | solution.py:521
  50.4 54.3 %collective-permute-start.8 = (bf16[256,2688]{1,0:T(8,128)(2,1)S(1)}, bf16[256,2688]{1,0:T(8,128)(2,1)S(1)}, u32[]{:S(2)}, u32[]{:S(2)}) collective-permute-start(bf16[256,2688]{1,0:T(8,128)(2,1)S(1)} %fusion.2.refs_0_), channel_id=1, source_target_pairs={{0,8},{1,9},{2,10},{3,11},{4,12},{5,13},{6,14},{7,15},{8,0},{9,1},... | collective-permute-start | bytes 4128776 | tf_op jit(solution)/shard_map/ppermute | solution.py:151
  52.0 54.6 %collective-permute-start.4 = (bf16[256,2688]{1,0:T(8,128)(2,1)S(1)}, bf16[256,2688]{1,0:T(8,128)(2,1)}, u32[]{:S(2)}, u32[]{:S(2)}) collective-permute-start(bf16[256,2688]{1,0:T(8,128)(2,1)S(1)} %fusion.2.refs_0_), channel_id=1, source_target_pairs={{0,4},{1,5},{2,6},{3,7},{4,0},{5,1},{6,2},{7,3},{8,12},{9,13},{10,... | collective-permute-start | bytes 4128776 | tf_op jit(solution)/shard_map/ppermute | solution.py:151
  52.7 54.8 %collective-permute-start.1 = (bf16[256,2688]{1,0:T(8,128)(2,1)S(1)}, bf16[256,2688]{1,0:T(8,128)(2,1)}, u32[]{:S(2)}, u32[]{:S(2)}) collective-permute-start(bf16[256,2688]{1,0:T(8,128)(2,1)S(1)} %fusion.2.refs_0_), channel_id=1, source_target_pairs={{0,1},{1,0},{2,3},{3,2},{4,5},{5,4},{6,7},{7,6},{8,9},{9,8},{10,11... | collective-permute-start | bytes 4128776 | tf_op jit(solution)/shard_map/ppermute | solution.py:151
  53.9 53.6 %collective-permute-start.2 = (bf16[256,2688]{1,0:T(8,128)(2,1)S(1)}, bf16[256,2688]{1,0:T(8,128)(2,1)}, u32[]{:S(2)}, u32[]{:S(2)}) collective-permute-start(bf16[256,2688]{1,0:T(8,128)(2,1)S(1)} %fusion.2.refs_0_), channel_id=1, source_target_pairs={{0,2},{1,3},{2,0},{3,1},{4,6},{5,7},{6,4},{7,5},{8,10},{9,11},{10,... | collective-permute-start | bytes 4128776 | tf_op jit(solution)/shard_map/ppermute | solution.py:151
  104.7 32.4 %collective-permute-start.12 = (bf16[256,2688]{1,0:T(8,128)(2,1)S(1)}, bf16[256,2688]{1,0:T(8,128)(2,1)}, u32[]{:S(2)}, u32[]{:S(2)}) collective-permute-start(bf16[256,2688]{1,0:T(8,128)(2,1)S(1)} %collective-permute-done.8.refs_8_), channel_id=1, source_target_pairs={{0,4},{1,5},{2,6},{3,7},{4,0},{5,1},{6,2},{7,3},{8,12},{9,13},{10,... | collective-permute-start | bytes 4128776 | tf_op jit(solution)/shard_map/ppermute | solution.py:151
  105.3 33.2 %collective-permute-start.9 = (bf16[256,2688]{1,0:T(8,128)(2,1)S(1)}, bf16[256,2688]{1,0:T(8,128)(2,1)}, u32[]{:S(2)}, u32[]{:S(2)}) collective-permute-start(bf16[256,2688]{1,0:T(8,128)(2,1)S(1)} %collective-permute-done.8.refs_8_), channel_id=1, source_target_pairs={{0,1},{1,0},{2,3},{3,2},{4,5},{5,4},{6,7},{7,6},{8,9},{9,8},{10,11... | collective-permute-start | bytes 4128776 | tf_op jit(solution)/shard_map/ppermute | solution.py:151
  106.6 61.4 %collective-permute-start.5 = (bf16[256,2688]{1,0:T(8,128)(2,1)}, bf16[256,2688]{1,0:T(8,128)(2,1)}, u32[]{:S(2)}, u32[]{:S(2)}) collective-permute-start(bf16[256,2688]{1,0:T(8,128)(2,1)} %collective-permute-done.4.refs_4_), channel_id=1, source_target_pairs={{0,1},{1,0},{2,3},{3,2},{4,5},{5,4},{6,7},{7,6},{8,9},{9,8},{10,11... | collective-permute-start | bytes 4128776 | tf_op jit(solution)/shard_map/ppermute | solution.py:151
  107.5 60.5 %collective-permute-start.10 = (bf16[256,2688]{1,0:T(8,128)(2,1)S(1)}, bf16[256,2688]{1,0:T(8,128)(2,1)}, u32[]{:S(2)}, u32[]{:S(2)}) collective-permute-start(bf16[256,2688]{1,0:T(8,128)(2,1)S(1)} %collective-permute-done.8.refs_8_), channel_id=1, source_target_pairs={{0,2},{1,3},{2,0},{3,1},{4,6},{5,7},{6,4},{7,5},{8,10},{9,11},{10,... | collective-permute-start | bytes 4128776 | tf_op jit(solution)/shard_map/ppermute | solution.py:151
  107.5 61.9 %collective-permute-start.6 = (bf16[256,2688]{1,0:T(8,128)(2,1)}, bf16[256,2688]{1,0:T(8,128)(2,1)}, u32[]{:S(2)}, u32[]{:S(2)}) collective-permute-start(bf16[256,2688]{1,0:T(8,128)(2,1)} %collective-permute-done.4.refs_4_), channel_id=1, source_target_pairs={{0,2},{1,3},{2,0},{3,1},{4,6},{5,7},{6,4},{7,5},{8,10},{9,11},{10,... | collective-permute-start | bytes 4128776 | tf_op jit(solution)/shard_map/ppermute | solution.py:151
  137.1 32.8 %collective-permute-start.3 = (bf16[256,2688]{1,0:T(8,128)(2,1)}, bf16[256,2688]{1,0:T(8,128)(2,1)}, u32[]{:S(2)}, u32[]{:S(2)}) collective-permute-start(bf16[256,2688]{1,0:T(8,128)(2,1)} %collective-permute-done.1.refs_1_), channel_id=1, source_target_pairs={{0,2},{1,3},{2,0},{3,1},{4,6},{5,7},{6,4},{7,5},{8,10},{9,11},{10,... | collective-permute-start | bytes 4128776 | tf_op jit(solution)/shard_map/ppermute | solution.py:151
  138.5 78.9 %collective-permute-start.13 = (bf16[256,2688]{1,0:T(8,128)(2,1)}, bf16[256,2688]{1,0:T(8,128)(2,1)}, u32[]{:S(2)}, u32[]{:S(2)}) collective-permute-start(bf16[256,2688]{1,0:T(8,128)(2,1)} %collective-permute-done.12.refs_12_), channel_id=1, source_target_pairs={{0,1},{1,0},{2,3},{3,2},{4,5},{5,4},{6,7},{7,6},{8,9},{9,8},{10,11... | collective-permute-start | bytes 4128776 | tf_op jit(solution)/shard_map/ppermute | solution.py:151
  168.0 10.9 %collective-permute-start.17 = (bf16[672,256]{1,0:T(8,128)(2,1)S(1)}, bf16[672,256]{1,0:T(8,128)(2,1)S(1)}, u32[]{:S(2)}, u32[]{:S(2)}) collective-permute-start(bf16[672,256]{1,0:T(8,128)(2,1)S(1)} %get-tuple-element.90), channel_id=1, source_target_pairs={{0,4},{1,5},{2,6},{3,7},{4,0},{5,1},{6,2},{7,3},{8,12},{9,13},{10,... | collective-permute-start | bytes 1032200 | tf_op jit(solution)/shard_map/ppermute | solution.py:151
  169.4 16.0 %collective-permute-start.18 = (bf16[672,256]{1,0:T(8,128)(2,1)S(1)}, bf16[672,256]{1,0:T(8,128)(2,1)S(1)}, u32[]{:S(2)}, u32[]{:S(2)}) collective-permute-start(bf16[672,256]{1,0:T(8,128)(2,1)S(1)} %get-tuple-element.89), channel_id=1, source_target_pairs={{0,6},{1,7},{2,4},{3,5},{4,2},{5,3},{6,0},{7,1},{8,14},{9,15},{10,... | collective-permute-start | bytes 1032200 | tf_op jit(solution)/shard_map/ppermute | solution.py:151
  169.9 47.5 %collective-permute-start.19 = (bf16[672,256]{1,0:T(8,128)(2,1)S(1)}, bf16[672,256]{1,0:T(8,128)(2,1)S(1)}, u32[]{:S(2)}, u32[]{:S(2)}) collective-permute-start(bf16[672,256]{1,0:T(8,128)(2,1)S(1)} %get-tuple-element.88), channel_id=1, source_target_pairs={{0,8},{1,9},{2,10},{3,11},{4,12},{5,13},{6,14},{7,15},{8,0},{9,1},... | collective-permute-start | bytes 1032200 | tf_op jit(solution)/shard_map/ppermute | solution.py:151
  169.9 109.4 %collective-permute-start.14 = (bf16[256,2688]{1,0:T(8,128)(2,1)}, bf16[256,2688]{1,0:T(8,128)(2,1)}, u32[]{:S(2)}, u32[]{:S(2)}) collective-permute-start(bf16[256,2688]{1,0:T(8,128)(2,1)} %collective-permute-done.12.refs_12_), channel_id=1, source_target_pairs={{0,2},{1,3},{2,0},{3,1},{4,6},{5,7},{6,4},{7,5},{8,10},{9,11},{10,... | collective-permute-start | bytes 4128776 | tf_op jit(solution)/shard_map/ppermute | solution.py:151
  178.9 100.4 %collective-permute-start.11 = (bf16[256,2688]{1,0:T(8,128)(2,1)}, bf16[256,2688]{1,0:T(8,128)(2,1)}, u32[]{:S(2)}, u32[]{:S(2)}) collective-permute-start(bf16[256,2688]{1,0:T(8,128)(2,1)} %collective-permute-done.9.refs_9_), channel_id=1, source_target_pairs={{0,2},{1,3},{2,0},{3,1},{4,6},{5,7},{6,4},{7,5},{8,10},{9,11},{10,... | collective-permute-start | bytes 4128776 | tf_op jit(solution)/shard_map/ppermute | solution.py:151
  185.4 93.9 %collective-permute-start.7 = (bf16[256,2688]{1,0:T(8,128)(2,1)}, bf16[256,2688]{1,0:T(8,128)(2,1)}, u32[]{:S(2)}, u32[]{:S(2)}) collective-permute-start(bf16[256,2688]{1,0:T(8,128)(2,1)} %collective-permute-done.5.refs_5_), channel_id=1, source_target_pairs={{0,2},{1,3},{2,0},{3,1},{4,6},{5,7},{6,4},{7,5},{8,10},{9,11},{10,... | collective-permute-start | bytes 4128776 | tf_op jit(solution)/shard_map/ppermute | solution.py:151
  217.4 61.9 %collective-permute-start.15 = (bf16[256,2688]{1,0:T(8,128)(2,1)}, bf16[256,2688]{1,0:T(8,128)(2,1)}, u32[]{:S(2)}, u32[]{:S(2)}) collective-permute-start(bf16[256,2688]{1,0:T(8,128)(2,1)} %collective-permute-done.13.refs_13_), channel_id=1, source_target_pairs={{0,2},{1,3},{2,0},{3,1},{4,6},{5,7},{6,4},{7,5},{8,10},{9,11},{10,... | collective-permute-start | bytes 4128776 | tf_op jit(solution)/shard_map/ppermute | solution.py:151
  217.4 16.8 %collective-permute-start.20 = (bf16[672,256]{1,0:T(8,128)(2,1)S(1)}, bf16[672,256]{1,0:T(8,128)(2,1)S(1)}, u32[]{:S(2)}, u32[]{:S(2)}) collective-permute-start(bf16[672,256]{1,0:T(8,128)(2,1)S(1)} %get-tuple-element.87), channel_id=1, source_target_pairs={{0,10},{1,11},{2,8},{3,9},{4,14},{5,15},{6,12},{7,13},{8,2},{9,3},... | collective-permute-start | bytes 1032200 | tf_op jit(solution)/shard_map/ppermute | solution.py:151
  235.0 32.4 %collective-permute-start.21 = (bf16[672,256]{1,0:T(8,128)(2,1)S(1)}, bf16[672,256]{1,0:T(8,128)(2,1)S(1)}, u32[]{:S(2)}, u32[]{:S(2)}) collective-permute-start(bf16[672,256]{1,0:T(8,128)(2,1)S(1)} %get-tuple-element.86), channel_id=1, source_target_pairs={{0,12},{1,13},{2,14},{3,15},{4,8},{5,9},{6,10},{7,11},{8,4},{9,5},... | collective-permute-start | bytes 1032200 | tf_op jit(solution)/shard_map/ppermute | solution.py:151
  267.4 11.2 %collective-permute-start.22 = (bf16[672,256]{1,0:T(8,128)(2,1)S(1)}, bf16[672,256]{1,0:T(8,128)(2,1)S(1)}, u32[]{:S(2)}, u32[]{:S(2)}) collective-permute-start(bf16[672,256]{1,0:T(8,128)(2,1)S(1)} %get-tuple-element.85), channel_id=1, source_target_pairs={{0,14},{1,15},{2,12},{3,13},{4,10},{5,11},{6,8},{7,9},{8,6},{9,7},... | collective-permute-start | bytes 1032200 | tf_op jit(solution)/shard_map/ppermute | solution.py:151
  298.0 13.4 %collective-permute-start.23 = (bf16[4,256,256]{2,1,0:T(8,128)(2,1)}, bf16[4,256,256]{2,1,0:T(8,128)(2,1)}, u32[]{:S(2)}, u32[]{:S(2)}) collective-permute-start(bf16[4,256,256]{2,1,0:T(8,128)(2,1)} %get-tuple-element.37), channel_id=1, source_target_pairs={{0,16},{1,17},{2,18},{3,19},{4,20},{5,21},{6,22},{7,23},{8,24},{9,... | collective-permute-start | bytes 1572872 | tf_op jit(solution)/shard_map/ppermute | solution.py:493
  346.4 16.6 %collective-permute-start.31 = (bf16[8,128,256]{2,1,0:T(8,128)(2,1)}, bf16[8,128,256]{2,1,0:T(8,128)(2,1)S(1)}, u32[]{:S(2)}, u32[]{:S(2)}) collective-permute-start(bf16[8,128,256]{2,1,0:T(8,128)(2,1)} %get-tuple-element.47), channel_id=1, source_target_pairs={{0,1},{1,0},{2,3},{3,2},{4,5},{5,4},{6,7},{7,6},{8,9},{9,8},{10,11... | collective-permute-start | bytes 1572872 | tf_op jit(solution)/shard_map/ppermute | solution.py:151
  348.9 26.5 %collective-permute-start.38 = (bf16[8,128,256]{2,1,0:T(8,128)(2,1)}, bf16[8,128,256]{2,1,0:T(8,128)(2,1)S(1)}, u32[]{:S(2)}, u32[]{:S(2)}) collective-permute-start(bf16[8,128,256]{2,1,0:T(8,128)(2,1)} %get-tuple-element.46.refs_0_), channel_id=1, source_target_pairs={{0,8},{1,9},{2,10},{3,11},{4,12},{5,13},{6,14},{7,15},{8,0},{9,1},... | collective-permute-start | bytes 1572872 | tf_op jit(solution)/shard_map/ppermute | solution.py:151
  361.5 15.0 %collective-permute-start.34 = (bf16[8,128,256]{2,1,0:T(8,128)(2,1)}, bf16[8,128,256]{2,1,0:T(8,128)(2,1)S(1)}, u32[]{:S(2)}, u32[]{:S(2)}) collective-permute-start(bf16[8,128,256]{2,1,0:T(8,128)(2,1)} %get-tuple-element.46.refs_0_), channel_id=1, source_target_pairs={{0,4},{1,5},{2,6},{3,7},{4,0},{5,1},{6,2},{7,3},{8,12},{9,13},{10,... | collective-permute-start | bytes 1572872 | tf_op jit(solution)/shard_map/ppermute | solution.py:151
  363.0 13.5 %collective-permute-start.32 = (bf16[8,128,256]{2,1,0:T(8,128)(2,1)}, bf16[8,128,256]{2,1,0:T(8,128)(2,1)S(1)}, u32[]{:S(2)}, u32[]{:S(2)}) collective-permute-start(bf16[8,128,256]{2,1,0:T(8,128)(2,1)} %get-tuple-element.46.refs_0_), channel_id=1, source_target_pairs={{0,2},{1,3},{2,0},{3,1},{4,6},{5,7},{6,4},{7,5},{8,10},{9,11},{10,... | collective-permute-start | bytes 1572872 | tf_op jit(solution)/shard_map/ppermute | solution.py:151
  363.0 24.7 %collective-permute-start.35 = (bf16[8,128,256]{2,1,0:T(8,128)(2,1)S(1)}, bf16[8,128,256]{2,1,0:T(8,128)(2,1)S(1)}, u32[]{:S(2)}, u32[]{:S(2)}) collective-permute-start(bf16[8,128,256]{2,1,0:T(8,128)(2,1)S(1)} %collective-permute-done.31.refs_1_), channel_id=1, source_target_pairs={{0,4},{1,5},{2,6},{3,7},{4,0},{5,1},{6,2},{7,3},{8,12},{9,13},{10,... | collective-permute-start | bytes 1572872 | tf_op jit(solution)/shard_map/ppermute | solution.py:151
  363.6 25.0 %collective-permute-start.39 = (bf16[8,128,256]{2,1,0:T(8,128)(2,1)S(1)}, bf16[8,128,256]{2,1,0:T(8,128)(2,1)S(1)}, u32[]{:S(2)}, u32[]{:S(2)}) collective-permute-start(bf16[8,128,256]{2,1,0:T(8,128)(2,1)S(1)} %collective-permute-done.31.refs_1_), channel_id=1, source_target_pairs={{0,8},{1,9},{2,10},{3,11},{4,12},{5,13},{6,14},{7,15},{8,0},{9,1},... | collective-permute-start | bytes 1572872 | tf_op jit(solution)/shard_map/ppermute | solution.py:151
  375.4 22.1 %collective-permute-start.42 = (bf16[8,128,256]{2,1,0:T(8,128)(2,1)S(1)}, bf16[8,128,256]{2,1,0:T(8,128)(2,1)S(1)}, u32[]{:S(2)}, u32[]{:S(2)}) collective-permute-start(bf16[8,128,256]{2,1,0:T(8,128)(2,1)S(1)} %collective-permute-done.38.refs_8_), channel_id=1, source_target_pairs={{0,4},{1,5},{2,6},{3,7},{4,0},{5,1},{6,2},{7,3},{8,12},{9,13},{10,... | collective-permute-start | bytes 1572872 | tf_op jit(solution)/shard_map/ppermute | solution.py:151
  376.5 21.0 %collective-permute-start.33 = (bf16[8,128,256]{2,1,0:T(8,128)(2,1)S(1)}, bf16[8,128,256]{2,1,0:T(8,128)(2,1)S(1)}, u32[]{:S(2)}, u32[]{:S(2)}) collective-permute-start(bf16[8,128,256]{2,1,0:T(8,128)(2,1)S(1)} %collective-permute-done.31.refs_1_), channel_id=1, source_target_pairs={{0,2},{1,3},{2,0},{3,1},{4,6},{5,7},{6,4},{7,5},{8,10},{9,11},{10,... | collective-permute-start | bytes 1572872 | tf_op jit(solution)/shard_map/ppermute | solution.py:151
  376.6 21.5 %collective-permute-start.36 = (bf16[8,128,256]{2,1,0:T(8,128)(2,1)S(1)}, bf16[8,128,256]{2,1,0:T(8,128)(2,1)S(1)}, u32[]{:S(2)}, u32[]{:S(2)}) collective-permute-start(bf16[8,128,256]{2,1,0:T(8,128)(2,1)S(1)} %collective-permute-done.34.refs_4_), channel_id=1, source_target_pairs={{0,2},{1,3},{2,0},{3,1},{4,6},{5,7},{6,4},{7,5},{8,10},{9,11},{10,... | collective-permute-start | bytes 1572872 | tf_op jit(solution)/shard_map/ppermute | solution.py:151
  387.8 10.9 %collective-permute-start.43 = (bf16[8,128,256]{2,1,0:T(8,128)(2,1)S(1)}, bf16[8,128,256]{2,1,0:T(8,128)(2,1)S(1)}, u32[]{:S(2)}, u32[]{:S(2)}) collective-permute-start(bf16[8,128,256]{2,1,0:T(8,128)(2,1)S(1)} %collective-permute-done.35.refs_5_), channel_id=1, source_target_pairs={{0,8},{1,9},{2,10},{3,11},{4,12},{5,13},{6,14},{7,15},{8,0},{9,1},... | collective-permute-start | bytes 1572872 | tf_op jit(solution)/shard_map/ppermute | solution.py:151
  388.6 18.7 %collective-permute-start.40 = (bf16[8,128,256]{2,1,0:T(8,128)(2,1)S(1)}, bf16[8,128,256]{2,1,0:T(8,128)(2,1)S(1)}, u32[]{:S(2)}, u32[]{:S(2)}) collective-permute-start(bf16[8,128,256]{2,1,0:T(8,128)(2,1)S(1)} %collective-permute-done.38.refs_8_), channel_id=1, source_target_pairs={{0,2},{1,3},{2,0},{3,1},{4,6},{5,7},{6,4},{7,5},{8,10},{9,11},{10,... | collective-permute-start | bytes 1572872 | tf_op jit(solution)/shard_map/ppermute | solution.py:151
  397.5 9.9 %collective-permute-start.37 = (bf16[8,128,256]{2,1,0:T(8,128)(2,1)S(1)}, bf16[8,128,256]{2,1,0:T(8,128)(2,1)}, u32[]{:S(2)}, u32[]{:S(2)}) collective-permute-start(bf16[8,128,256]{2,1,0:T(8,128)(2,1)S(1)} %collective-permute-done.35.refs_5_), channel_id=1, source_target_pairs={{0,2},{1,3},{2,0},{3,1},{4,6},{5,7},{6,4},{7,5},{8,10},{9,11},{10,... | collective-permute-start | bytes 1572872 | tf_op jit(solution)/shard_map/ppermute | solution.py:151
  397.5 9.9 %collective-permute-start.41 = (bf16[8,128,256]{2,1,0:T(8,128)(2,1)S(1)}, bf16[8,128,256]{2,1,0:T(8,128)(2,1)}, u32[]{:S(2)}, u32[]{:S(2)}) collective-permute-start(bf16[8,128,256]{2,1,0:T(8,128)(2,1)S(1)} %collective-permute-done.39.refs_9_), channel_id=1, source_target_pairs={{0,2},{1,3},{2,0},{3,1},{4,6},{5,7},{6,4},{7,5},{8,10},{9,11},{10,... | collective-permute-start | bytes 1572872 | tf_op jit(solution)/shard_map/ppermute | solution.py:151
  398.1 9.3 %collective-permute-start.44 = (bf16[8,128,256]{2,1,0:T(8,128)(2,1)S(1)}, bf16[8,128,256]{2,1,0:T(8,128)(2,1)}, u32[]{:S(2)}, u32[]{:S(2)}) collective-permute-start(bf16[8,128,256]{2,1,0:T(8,128)(2,1)S(1)} %collective-permute-done.42.refs_12_), channel_id=1, source_target_pairs={{0,2},{1,3},{2,0},{3,1},{4,6},{5,7},{6,4},{7,5},{8,10},{9,11},{10,... | collective-permute-start | bytes 1572872 | tf_op jit(solution)/shard_map/ppermute | solution.py:151
  429.7 8.5 %collective-permute-start.56 = (bf16[128,336]{1,0:T(8,128)(2,1)}, bf16[128,336]{1,0:T(8,128)(2,1)S(1)}, u32[]{:S(2)}, u32[]{:S(2)}) collective-permute-start(bf16[128,336]{1,0:T(8,128)(2,1)} %get-tuple-element.60), channel_id=1, source_target_pairs={{0,9},{1,8},{2,11},{3,10},{4,13},{5,12},{6,15},{7,14},{8,1},{9,0},... | collective-permute-start | bytes 258056 | tf_op jit(solution)/shard_map/ppermute | solution.py:151
  430.8 9.6 %collective-permute-start.57 = (bf16[128,336]{1,0:T(8,128)(2,1)}, bf16[128,336]{1,0:T(8,128)(2,1)S(1)}, u32[]{:S(2)}, u32[]{:S(2)}) collective-permute-start(bf16[128,336]{1,0:T(8,128)(2,1)} %get-tuple-element.61), channel_id=1, source_target_pairs={{0,7},{1,6},{2,5},{3,4},{4,3},{5,2},{6,1},{7,0},{8,15},{9,14},{10,... | collective-permute-start | bytes 258056 | tf_op jit(solution)/shard_map/ppermute | solution.py:151
  432.2 11.0 %collective-permute-start.58 = (bf16[128,336]{1,0:T(8,128)(2,1)}, bf16[128,336]{1,0:T(8,128)(2,1)S(1)}, u32[]{:S(2)}, u32[]{:S(2)}) collective-permute-start(bf16[128,336]{1,0:T(8,128)(2,1)} %get-tuple-element.62), channel_id=1, source_target_pairs={{0,5},{1,4},{2,7},{3,6},{4,1},{5,0},{6,3},{7,2},{8,13},{9,12},{10,... | collective-permute-start | bytes 258056 | tf_op jit(solution)/shard_map/ppermute | solution.py:151
  434.9 9.5 %collective-permute-start.59 = (bf16[128,336]{1,0:T(8,128)(2,1)}, bf16[128,336]{1,0:T(8,128)(2,1)S(1)}, u32[]{:S(2)}, u32[]{:S(2)}) collective-permute-start(bf16[128,336]{1,0:T(8,128)(2,1)} %get-tuple-element.63), channel_id=1, source_target_pairs={{0,3},{1,2},{2,1},{3,0},{4,7},{5,6},{6,5},{7,4},{8,11},{9,10},{10,... | collective-permute-start | bytes 258056 | tf_op jit(solution)/shard_map/ppermute | solution.py:151
  435.6 11.1 %collective-permute-start.60 = (bf16[128,336]{1,0:T(8,128)(2,1)}, bf16[128,336]{1,0:T(8,128)(2,1)S(1)}, u32[]{:S(2)}, u32[]{:S(2)}) collective-permute-start(bf16[128,336]{1,0:T(8,128)(2,1)} %get-tuple-element.64), channel_id=1, source_target_pairs={{0,1},{1,0},{2,3},{3,2},{4,5},{5,4},{6,7},{7,6},{8,9},{9,8},{10,11... | collective-permute-start | bytes 258056 | tf_op jit(solution)/shard_map/ppermute | solution.py:151
  438.2 9.0 %collective-permute-start.46 = (bf16[128,336]{1,0:T(8,128)(2,1)}, bf16[128,336]{1,0:T(8,128)(2,1)S(1)}, u32[]{:S(2)}, u32[]{:S(2)}) collective-permute-start(bf16[128,336]{1,0:T(8,128)(2,1)} %get-tuple-element.49), channel_id=1, source_target_pairs={{0,14},{1,15},{2,12},{3,13},{4,10},{5,11},{6,8},{7,9},{8,6},{9,7},... | collective-permute-start | bytes 258056 | tf_op jit(solution)/shard_map/ppermute | solution.py:151
  (50 other events, 758.7 us)
Sparse Core Ops, SparseCore 0:
  11.1 73.6 all-gather.4
  86.3 69.8 all-gather.6
  158.1 107.5 all-gather.8
